TPU v7x, 256 devices: a whole 4x4x8 slice. The times are simulated.
256 devices in a mesh: gx: 16 (over z_hi, x), gy: 16 (over z_lo, y, core).
Axes of the slice: x: 4, y: 4, z: 8 (z_hi: 4, z_lo: 2; z = z_hi * 2 + z_lo), core: 2. Of those that a mesh axis runs over, the one named last changes fastest.
Arguments:
- moving_image: bfloat16 [16, 512, 4096], P(None, 'gx', 'gy'), may hold values from -6 to 6, as said below
- fixed_image: bfloat16 [16, 512, 4096], P(None, 'gx', 'gy'), may hold values from -6 to 6, as said below
- velocity: float32 [3, 16, 512, 4096], P(None, None, 'gx', 'gy'), may hold values from 0 to 1
- offsets: int32 [3, 32, 32], P(None, 'gx', 'gy'), may hold values from -7 to 7, as said below
- tissue: int32 [32, 32], P('gx', 'gy'), may hold values from 0 to 1, as said below
Outputs:
- update: float32 [3, 16, 512, 4096], P(None, None, 'gx', 'gy')
- similarity_loss: float32 [], replicated
Inputs may be any that keep to these rules, and one draw needn't show every extreme that they name: `moving_image`: the images stay within -6 to 6. `fixed_image`: the images stay within -6 to 6. `offsets`: channel 0 lies in -2 to 2, channels 1 and 2 in -7 to 7; each end is taken by some block. 1 marks a block that holds tissue; some blocks hold tissue.
All inputs are finite; a program needn't handle non-finite values.
Results may differ from a plain program's by a relative error of at most 0.0011.
Values may be sent and summed in bfloat16 or wider, within the bound.
No kernel may reach another device: no remote copies, remote signals or barrier semaphores. Data moves between devices by JAX's collectives and lax.ppermute only.
A program may use at most 64 MiB of HBM per device.

v0:
```python
import functools
import math

import jax
import jax.numpy as jnp
import numpy as np
from jax import lax
from jax.experimental import pallas as pl
from jax.experimental.pallas import tpu as pltpu
from jax.sharding import PartitionSpec as P

DEPTH = 16
BX = 16
BY = 128
ROWS = 32
EXT = 48
OUT = 40
LANES = 128
GAUSS_RADIUS = 7
GAUSS_SIGMA = 3.0
WINDOW_COUNT = 729.0
VAR_EPSILON = 1e-05
STEP_RATE = 16.0
F32 = jnp.float32
BF16 = jnp.bfloat16

VMEM_SPEC = pl.BlockSpec(memory_space=pltpu.VMEM)
SMEM_SPEC = pl.BlockSpec(memory_space=pltpu.SMEM)
ANY_SPEC = pl.BlockSpec(memory_space=pl.ANY)

PX, PY, HAS_L, HAS_R, OFF, TIS = 0, 1, 2, 3, 4, 16


def gauss_weights():
    raw = [
        math.exp(-float(tap * tap) / (2.0 * GAUSS_SIGMA * GAUSS_SIGMA))
        for tap in range(-GAUSS_RADIUS, GAUSS_RADIUS + 1)
    ]
    total = sum(raw)
    return [w / total for w in raw]


def lane_iota(shape):
    return lax.broadcasted_iota(jnp.int32, shape, len(shape) - 1)


def roll(x, shift):
    shift = shift % LANES
    return x if shift == 0 else pltpu.roll(x, shift, len(x.shape) - 1)


def pack_edge(tile, groups, last):
    rows = tile.shape[0] // groups
    width = LANES // groups
    lane = lane_iota((rows, LANES))
    acc = None
    for k in range(groups):
        piece = roll(tile[k * rows : (k + 1) * rows], width * (k + 1) if last else width * k)
        acc = piece if acc is None else jnp.where(lane // width == k, piece, acc)
    return acc


def unpack_group(right, left, k, groups):
    width = LANES // groups
    r = roll(right, -width * k)
    l = roll(left, -width * (k + 1))
    return jnp.where(lane_iota(r.shape) < LANES // 2, r, l)


def pick(flag, a, b):
    return jnp.where(flag == 0, a, b)


def planes(x, rows):
    return x.reshape(DEPTH, rows, x.shape[-1])


def edge_x_kernel(s_ref, m_ref, f_ref, e_ref, o_ref):
    px = s_ref[PX]
    lane = lane_iota((16, 2 * LANES))
    for n, ref in enumerate((m_ref, f_ref)):
        v = planes(ref[...].astype(F32), ROWS)
        first = v[:, :8].reshape(128, 2 * LANES)
        last = v[:, 24:].reshape(128, 2 * LANES)
        e_ref[128 * n : 128 * n + 128] = pick(px, last, first).astype(BF16)
        o_ref[128 * n : 128 * n + 128] = pick(px, first, last).astype(BF16)
    t = [[s_ref[TIS + 2 * i + j].astype(F32) for j in range(2)] for i in range(2)]
    first = jnp.where(lane < LANES, t[0][0], t[0][1])
    last = jnp.where(lane < LANES, t[1][0], t[1][1])
    e_ref[256:272] = pick(px, last, first).astype(BF16)
    o_ref[256:272] = pick(px, first, last).astype(BF16)


def edge_v_kernel(s_ref, v_ref, e_ref, o_ref):
    py = s_ref[PY]
    for c in range(3):
        first = pack_edge(v_ref[c, :, :LANES], 8, False)
        last = pack_edge(v_ref[c, :, LANES:], 8, True)
        for ref, val in ((e_ref, pick(py, last, first)), (o_ref, pick(py, first, last))):
            hi = val.astype(BF16)
            ref[128 * c : 128 * c + 64] = hi
            ref[128 * c + 64 : 128 * c + 128] = (val - hi.astype(F32)).astype(BF16)


def before_after(px, e, o):
    return pick(px, o, e), pick(px, e, o)


def extended(own, e_ref, o_ref, px, base):
    e = e_ref[base : base + 128].astype(F32)
    o = o_ref[base : base + 128].astype(F32)
    before, after = before_after(px, e, o)
    return jnp.concatenate(
        [planes(before, 8), planes(own.astype(F32), ROWS), planes(after, 8)], axis=1
    )


def edge_y_kernel(s_ref, m_ref, f_ref, xe_ref, xo_ref, ve_ref, vo_ref, e_ref, o_ref):
    px = s_ref[PX]
    py = s_ref[PY]
    row = 0
    for n, (ref, groups) in enumerate(((m_ref, 4), (f_ref, 8))):
        ext = extended(ref[...], xe_ref, xo_ref, px, 128 * n).reshape(DEPTH * EXT, 2 * LANES)
        first = pack_edge(ext[:, :LANES], groups, False)
        last = pack_edge(ext[:, LANES:], groups, True)
        size = first.shape[0]
        e_ref[row : row + size] = pick(py, last, first).astype(BF16)
        o_ref[row : row + size] = pick(py, first, last).astype(BF16)
        row += size
    e_ref[row : row + 384] = ve_ref[...]
    o_ref[row : row + 384] = vo_ref[...]
    row += 384
    before, after = before_after(px, xe_ref[256:272].astype(F32), xo_ref[256:272].astype(F32))
    lane = lane_iota((16, LANES))
    sides = []
    for j in range(2):
        acc = jnp.zeros((16, LANES), F32)
        for c in range(3):
            for i in range(2):
                acc = jnp.where(lane == 2 * c + i, s_ref[OFF + 4 * c + 2 * i + j].astype(F32), acc)
        tissue = (
            before[:, LANES * j : LANES * j + LANES],
            s_ref[TIS + j].astype(F32),
            s_ref[TIS + 2 + j].astype(F32),
            after[:, LANES * j : LANES * j + LANES],
        )
        for i, t in enumerate(tissue):
            acc = jnp.where(lane == 8 + i, t, acc)
        sides.append(acc)
    e_ref[row : row + 16] = pick(py, sides[1], sides[0]).astype(BF16)
    o_ref[row : row + 16] = pick(py, sides[0], sides[1]).astype(BF16)


Y_FIXED, Y_VEL, Y_META, Y_ROWS = 192, 288, 672, 688


def sides_of(py, e_ref, o_ref, start, size):
    e = e_ref[start : start + size].astype(F32)
    o = o_ref[start : start + size].astype(F32)
    left, right = before_after(py, e, o)
    return right, left


def warp_kernel(
    s_ref, m_ref, xe_ref, xo_ref, ye_ref, yo_ref, v_hbm,
    w_ref, slope_ref, e_ref, o_ref,
    m_scr, v_scr, r_scr, sem,
):
    px = s_ref[PX]
    py = s_ref[PY]
    copies = []
    for c in range(3):
        for j in range(2):
            copies.append(
                pltpu.make_async_copy(
                    v_hbm.at[c, :, pl.ds(LANES * j, LANES)], v_scr.at[c, j], sem.at[2 * c + j]
                )
            )
    for copy in copies:
        copy.start()

    zero = jnp.zeros((3 * EXT, LANES), F32)
    for j in range(3):
        m_scr[j, 0 : 3 * EXT] = zero
        m_scr[j, 19 * EXT : 22 * EXT] = zero
    ext = extended(m_ref[...], xe_ref, xo_ref, px, 0).reshape(DEPTH * EXT, 2 * LANES)
    m_scr[0, 3 * EXT : 19 * EXT] = ext[:, :LANES]
    m_scr[1, 3 * EXT : 19 * EXT] = ext[:, LANES:]
    right, left = sides_of(py, ye_ref, yo_ref, 0, 192)
    for k in range(4):
        m_scr[2, 3 * EXT + 192 * k : 3 * EXT + 192 * k + 192] = unpack_group(right, left, k, 4)
    for c in range(3):
        right, left = sides_of(py, ye_ref, yo_ref, Y_VEL + 128 * c, 128)
        right = right[:64] + right[64:]
        left = left[:64] + left[64:]
        for k in range(8):
            v_scr[c, 2, 64 * k : 64 * k + 64] = unpack_group(right, left, k, 8)
    m_right, m_left = sides_of(py, ye_ref, yo_ref, Y_META, 16)
    lane8 = lane_iota((16, LANES))
    first_row = lax.broadcasted_iota(jnp.int32, (16, LANES), 0) == 0

    def scalar(meta, k):
        return jnp.sum(jnp.where(first_row & (lane8 == k), meta, 0.0)).astype(jnp.int32)

    lane = lane_iota((DEPTH, LANES))

    def gather(j, xb, oz, ox, oy, merge):
        shifts = []
        for b in range(2):
            s = oy + b
            nbr = jnp.where(s >= 0, (j + 1) % 3, (j + 2) % 3)
            lo = jnp.where(s >= 0, 0, LANES + s)
            hi = jnp.where(s >= 0, s, LANES)
            mask = (lane >= lo) & (lane < hi)
            shifts.append((nbr, mask, (LANES - s) & (LANES - 1)))
        base = (3 + oz) * EXT + xb * BX + 8 + ox

        @pl.loop(0, BX + 1)
        def _(x):
            for c in range(2):
                start = base + c * EXT + x
                own = m_scr[j, pl.ds(start, DEPTH, stride=EXT), :]
                for b in range(2):
                    nbr, mask, amount = shifts[b]
                    other = m_scr[nbr, pl.ds(start, DEPTH, stride=EXT), :]
                    val = pltpu.roll(jnp.where(mask, other, own), amount, 1)
                    if merge:
                        val = jnp.where(lane < LANES // 2, r_scr[b, c, x], val)
                    r_scr[b, c, x] = val

    def blend(j, xb):
        @pl.loop(0, BX)
        def _(x):
            row = xb * BX + x
            f0, f1, f2 = (v_scr[c, j, pl.ds(row, DEPTH, stride=ROWS), :] for c in range(3))
            mid, dx, dy = [], [], []
            for c in range(2):
                low, dif = [], []
                for a in range(2):
                    s0 = r_scr[0, c, x + a]
                    d = r_scr[1, c, x + a] - s0
                    dif.append(d)
                    low.append(s0 + f2 * d)
                step = low[1] - low[0]
                dx.append(step)
                mid.append(low[0] + f1 * step)
                dy.append(dif[0] + f1 * (dif[1] - dif[0]))
            dz = mid[1] - mid[0]
            lanes = slice(LANES * j, LANES * j + LANES)
            w_ref[row, :, lanes] = (mid[0] + f0 * dz).astype(BF16)
            slope_ref[0, row, :, lanes] = dz
            slope_ref[1, row, :, lanes] = dx[0] + f0 * (dx[1] - dx[0])
            slope_ref[2, row, :, lanes] = dy[0] + f0 * (dy[1] - dy[0])

    for xb in range(2):
        gather(2, xb, *(scalar(m_right, 2 * c + xb) for c in range(3)), False)
        gather(2, xb, *(scalar(m_left, 2 * c + xb) for c in range(3)), True)
        blend(2, xb)
    for copy in copies:
        copy.wait()
    for j in range(2):
        for xb in range(2):
            gather(j, xb, *(s_ref[OFF + 4 * c + 2 * xb + j] for c in range(3)), False)
            blend(j, xb)
    e_ref[...] = w_ref[pl.ds(jnp.where(px == 0, ROWS - 8, 0), 8)]
    o_ref[...] = w_ref[pl.ds(jnp.where(px == 0, 0, ROWS - 8), 8)]


def box_x(load, store, count):
    v, three = {}, {}
    for x in range(count + 8):
        v[x] = load(x)
        if x >= 2:
            three[x - 2] = v[x - 2] + v[x - 1] + v[x]
        if x >= 8:
            store(x - 8, three[x - 8] + three[x - 5] + three[x - 2])


def add_all(terms):
    terms = [t for t in terms if t is not None]
    if not terms:
        return None
    total = terms[0]
    for t in terms[1:]:
        total = total + t
    return total


def box_z(v):
    three = {z: add_all([v[i] for i in (z - 1, z, z + 1) if 0 <= i < DEPTH]) for z in range(-3, 19)}
    return [add_all([three[z - 3], three[z], three[z + 3]]) for z in range(DEPTH)]


def shift_y(v, s):
    lane = lane_iota(v[0].shape)
    if s > 0:
        return [roll(jnp.where(lane < s, v[(j + 1) % 3], v[j]), -s) for j in range(3)]
    return [roll(jnp.where(lane >= LANES + s, v[(j + 2) % 3], v[j]), -s) for j in range(3)]


def box_y(v):
    for s in (1, 3):
        a, b = shift_y(v, s), shift_y(v, -s)
        v = [x + y + z for x, y, z in zip(a, v, b)]
    return v


def fixed_kernel(
    s_ref, f_ref, xe_ref, xo_ref, ye_ref, yo_ref,
    fx_ref, sum_ref, mask_ref,
    f_scr, z_scr, b_scr,
):
    px = s_ref[PX]
    py = s_ref[PY]
    ext = extended(f_ref[...], xe_ref, xo_ref, px, 128).reshape(DEPTH * EXT, 2 * LANES)
    f_scr[0] = ext[:, :LANES]
    f_scr[1] = ext[:, LANES:]
    right, left = sides_of(py, ye_ref, yo_ref, Y_FIXED, 96)
    for k in range(8):
        f_scr[2, 96 * k : 96 * k + 96] = unpack_group(right, left, k, 8)

    before, after = before_after(px, xe_ref[256:264].astype(F32), xo_ref[256:264].astype(F32))
    m_right, m_left = sides_of(py, ye_ref, yo_ref, Y_META, 8)
    row = lax.broadcasted_iota(jnp.int32, (OUT, LANES), 0)
    lane = lane_iota((8, LANES))

    def column(meta, k):
        picked = jnp.sum(jnp.where(lane == 8 + k, meta, 0.0), axis=1, keepdims=True)[:1]
        return jnp.broadcast_to(picked, (1, LANES))

    for j in range(3):
        if j < 2:
            lanes = slice(LANES * j, LANES * j + LANES)
            t = [
                before[:1, lanes],
                jnp.full((1, LANES), s_ref[TIS + j].astype(F32)),
                jnp.full((1, LANES), s_ref[TIS + 2 + j].astype(F32)),
                after[:1, lanes],
            ]
        else:
            half = lane_iota((1, LANES)) < LANES // 2
            t = [jnp.where(half, column(m_right, k), column(m_left, k)) for k in range(4)]
        mask_ref[j] = jnp.where(row < 4, t[0], jnp.where(row < 20, t[1], jnp.where(row < 36, t[2], t[3])))

    @pl.loop(0, 3)
    def _(j):
        def load(x):
            return f_scr[j, pl.ds(x, DEPTH, stride=EXT), :]

        for q in range(2):
            def value(x):
                v = load(x)
                if q == 0:
                    fx_ref[x, j] = v.astype(BF16)
                return v if q == 0 else v * v

            def store(x, v):
                z_scr[q, j, pl.ds(x, DEPTH, stride=OUT), :] = v

            box_x(value, store, OUT)

    sum_zy(z_scr, b_scr, 2, lambda z, at, sums: put_sums(sum_ref, at, sums))


def put_sums(ref, at, sums):
    for q, v in enumerate(sums):
        for j in range(3):
            ref[q, j, pl.ds(at, 8), :] = v[j]


def sum_zy(z_scr, b_scr, count, use):
    @pl.loop(0, OUT // 8)
    def _(t):
        def at(z):
            return pl.multiple_of(z * OUT + t * 8, 8)

        for q in range(count):
            for j in range(3):
                v = box_z([z_scr[q, j, pl.ds(at(z), 8), :] for z in range(DEPTH)])
                for z in range(DEPTH):
                    b_scr[q, j, z] = v[z]

        @pl.loop(0, DEPTH)
        def _(z):
            use(t, at(z), [box_y([b_scr[q, j, z] for j in range(3)]) for q in range(count)])


def gradient_kernel(
    s_ref, w_ref, we_ref, wo_ref, fx_ref, sum_ref, mask_ref, slope_ref, gh_ref, gl_ref,
    ys_ref, e_ref, o_ref, loss_ref,
    i_scr, z_scr, b_scr, a_scr, g_scr,
):
    px = s_ref[PX]
    before, after = before_after(px, we_ref[...].astype(F32), wo_ref[...].astype(F32))
    for j in range(3):
        lanes = slice(LANES * j, LANES * j + LANES)
        i_scr[0:8, j] = before[:, :, lanes]
        i_scr[8:40, j] = w_ref[:, :, lanes].astype(F32)
        i_scr[40:48, j] = after[:, :, lanes]

    @pl.loop(0, 3)
    def _(j):
        for q in range(3):
            def value(x):
                v = i_scr[x, j]
                if q == 0:
                    return v
                return v * (v if q == 1 else fx_ref[x, j].astype(F32))

            def store(x, v):
                z_scr[q, j, pl.ds(x, DEPTH, stride=OUT), :] = v

            box_x(value, store, OUT)

    loss_ref[...] = jnp.zeros((8, LANES), F32)
    rows8 = lax.broadcasted_iota(jnp.int32, (8, LANES), 0)

    def stats(t, at, sums):
        inner = (rows8 + t * 8 >= 4) & (rows8 + t * 8 < 4 + ROWS)
        total = None
        for j in range(3):
            si, sii, sij = (sums[q][j] for q in range(3))
            sj = sum_ref[0, j, pl.ds(at, 8), :]
            sjj = sum_ref[1, j, pl.ds(at, 8), :]
            m = mask_ref[j, pl.ds(pl.multiple_of(t * 8, 8), 8), :]
            cross = sij - si * sj * (1.0 / WINDOW_COUNT)
            var_i = sii - si * si * (1.0 / WINDOW_COUNT)
            var_j = sjj - sj * sj * (1.0 / WINDOW_COUNT)
            quotient = cross / (var_i * var_j + VAR_EPSILON)
            second = quotient * quotient * var_j
            a_scr[0, j, pl.ds(at, 8), :] = (2.0 / WINDOW_COUNT) * m * (quotient * sj - second * si)
            a_scr[1, j, pl.ds(at, 8), :] = m * second
            a_scr[2, j, pl.ds(at, 8), :] = -2.0 * m * quotient
            if j < 2:
                ncc = jnp.where(inner, m * (cross * quotient), 0.0)
                total = ncc if total is None else total + ncc
        loss_ref[...] += total

    sum_zy(z_scr, b_scr, 3, stats)
    sum_zy(a_scr, b_scr, 3, lambda t, at, sums: put_sums(z_scr, at, sums))

    lane = lane_iota((DEPTH, LANES))
    has_r = s_ref[HAS_R]
    has_l = s_ref[HAS_L]
    r_lim = jnp.where(has_r == 1, GAUSS_RADIUS, 0)
    l_lim = jnp.where(has_l == 1, LANES - GAUSS_RADIUS, LANES)
    valid = (lane < r_lim) | (lane >= l_lim)

    for j in range(3):
        lanes = slice(LANES * j, LANES * j + LANES)
        for q in range(3):
            def load(x):
                return z_scr[q, j, pl.ds(x, DEPTH, stride=OUT), :]

            def store(x, v):
                if q == 0:
                    g_scr[0, x, :, lanes] = v
                elif q == 1:
                    g_scr[0, x, :, lanes] += 2.0 * i_scr[x + 8, j] * v
                else:
                    grad = g_scr[0, x, :, lanes] + fx_ref[x + 8, j].astype(F32) * v
                    for c in (2, 1, 0):
                        val = grad * slope_ref[c, x, :, lanes]
                        if j == 2:
                            val = jnp.where(valid, val, 0.0)
                        g_scr[c, x, :, lanes] = val

            box_x(load, store, ROWS)

    gh = gh_ref[...]
    gl = gl_ref[...]
    for c in range(3):
        g = g_scr[c].reshape(ROWS * DEPTH, 3 * LANES)
        hi = g.astype(BF16)
        lo = (g - hi.astype(F32)).astype(BF16)
        ys = jnp.dot(hi, gh, preferred_element_type=F32)
        ys = ys + jnp.dot(lo, gh, preferred_element_type=F32)
        ys = ys + jnp.dot(hi, gl, preferred_element_type=F32)
        ys = ys.reshape(ROWS, DEPTH, 2 * LANES)
        ys_ref[c] = ys
        first = ys[:GAUSS_RADIUS]
        last = ys[ROWS - GAUSS_RADIUS :]
        e_ref[c] = pick(px, last, first).astype(BF16)
        o_ref[c] = pick(px, first, last).astype(BF16)


def smooth_kernel(s_ref, ys_ref, ge_ref, go_ref, out_hbm, h_scr, z_scr, o_scr, sem):
    weights = gauss_weights()
    px = s_ref[PX]
    r = GAUSS_RADIUS
    for c in range(3):
        before, after = before_after(px, ge_ref[c].astype(F32), go_ref[c].astype(F32))
        h_scr[0, c] = before
        h_scr[1, c] = after
    copies = []
    for c in range(3):
        for j in range(2):
            lanes = slice(LANES * j, LANES * j + LANES)

            def load(x):
                if x < r:
                    return h_scr[0, c, x, :, lanes]
                if x < r + ROWS:
                    return ys_ref[c, x - r, :, lanes]
                return h_scr[1, c, x - r - ROWS, :, lanes]

            for x in range(ROWS):
                total = (-STEP_RATE * weights[r]) * load(x + r)
                for k in range(1, r + 1):
                    total = total + (-STEP_RATE * weights[r + k]) * (load(x + r - k) + load(x + r + k))
                z_scr[pl.ds(x, DEPTH, stride=ROWS), :] = total

            @pl.loop(0, ROWS // 8)
            def _(t):
                def at(z):
                    return pl.multiple_of(z * ROWS + t * 8, 8)

                v = [z_scr[pl.ds(at(z), 8), :] for z in range(DEPTH)]
                for z in range(DEPTH):
                    total = weights[r] * v[z]
                    for k in range(1, r + 1):
                        pair = add_all([v[i] for i in (z - k, z + k) if 0 <= i < DEPTH])
                        if pair is not None:
                            total = total + weights[r + k] * pair
                    o_scr[c, j, pl.ds(at(z), 8), :] = total

            copy = pltpu.make_async_copy(
                o_scr.at[c, j], out_hbm.at[c, :, pl.ds(LANES * j, LANES)], sem.at[2 * c + j]
            )
            copy.start()
            copies.append(copy)
    for copy in copies:
        copy.wait()


def call(kernel, outs, in_specs, out_specs, scratch=()):
    return pl.pallas_call(
        kernel,
        out_shape=tuple(jax.ShapeDtypeStruct(s, d) for s, d in outs),
        in_specs=list(in_specs),
        out_specs=tuple(out_specs),
        scratch_shapes=list(scratch),
        name=kernel.__name__,
    )


def swap(axis, even, odd):
    count = lax.axis_size(axis)
    first = [(i, i ^ 1) for i in range(count) if i ^ 1 < count]
    second = []
    for i in range(1, count - 1, 2):
        second += [(i, i + 1), (i + 1, i)]
    return lax.ppermute(even, axis, first), lax.ppermute(odd, axis, second)


def gauss_matrices():
    weights = gauss_weights()
    g = np.zeros((3 * LANES, 2 * LANES), np.float32)
    for col in range(2 * LANES):
        for tap in range(-GAUSS_RADIUS, GAUSS_RADIUS + 1):
            g[(col + tap) % (3 * LANES), col] = weights[tap + GAUSS_RADIUS]
    hi = jnp.asarray(g).astype(BF16)
    lo = (jnp.asarray(g) - hi.astype(F32)).astype(BF16)
    return hi, lo


def on_device(moving_image, fixed_image, velocity, offsets, tissue):
    ix, iy = lax.axis_index("gx"), lax.axis_index("gy")
    ny = lax.axis_size("gy")
    table = jnp.concatenate(
        [
            jnp.stack([ix & 1, iy & 1, (iy > 0).astype(jnp.int32), (iy < ny - 1).astype(jnp.int32)]),
            offsets.reshape(12),
            tissue.reshape(4),
        ]
    ).astype(jnp.int32)
    rows = DEPTH * ROWS
    m = moving_image.reshape(rows, 2 * LANES)
    f = fixed_image.reshape(rows, 2 * LANES)
    v = velocity.reshape(3, rows, 2 * LANES)

    V, S, A = VMEM_SPEC, SMEM_SPEC, ANY_SPEC
    edge = ((272, 2 * LANES), BF16)
    xe, xo = call(edge_x_kernel, [edge, edge], [S, V, V], [V, V])(table, m, f)
    rxe, rxo = swap("gx", xe, xo)
    edge = ((384, LANES), BF16)
    ve, vo = call(edge_v_kernel, [edge, edge], [S, V], [V, V])(table, v)
    edge = ((Y_ROWS, LANES), BF16)
    ye, yo = call(edge_y_kernel, [edge, edge], [S] + [V] * 6, [V, V])(table, m, f, rxe, rxo, ve, vo)
    rye, ryo = swap("gy", ye, yo)

    edge = ((8, DEPTH, 3 * LANES), BF16)
    w, slope, we, wo = call(
        warp_kernel,
        [((ROWS, DEPTH, 3 * LANES), BF16), ((3, ROWS, DEPTH, 3 * LANES), F32), edge, edge],
        [S] + [V] * 5 + [A],
        [V] * 4,
        [
            pltpu.VMEM((3, 22 * EXT, LANES), F32),
            pltpu.VMEM((3, 3, rows, LANES), F32),
            pltpu.VMEM((2, 2, BX + 1, DEPTH, LANES), F32),
            pltpu.SemaphoreType.DMA((6,)),
        ],
    )(table, m, rxe, rxo, rye, ryo, v)
    rwe, rwo = swap("gx", we, wo)

    fx, sums, mask = call(
        fixed_kernel,
        [((EXT, 3, DEPTH, LANES), BF16), ((2, 3, DEPTH * OUT, LANES), F32), ((3, OUT, LANES), F32)],
        [S] + [V] * 5,
        [V] * 3,
        [
            pltpu.VMEM((3, DEPTH * EXT, LANES), F32),
            pltpu.VMEM((2, 3, DEPTH * OUT, LANES), F32),
            pltpu.VMEM((2, 3, DEPTH, 8, LANES), F32),
        ],
    )(table, f, rxe, rxo, rye, ryo)

    gh, gl = gauss_matrices()
    edge = ((3, GAUSS_RADIUS, DEPTH, 2 * LANES), BF16)
    ys, ge, go, loss = call(
        gradient_kernel,
        [((3, ROWS, DEPTH, 2 * LANES), F32), edge, edge, ((8, LANES), F32)],
        [S] + [V] * 9,
        [V] * 4,
        [
            pltpu.VMEM((EXT, 3, DEPTH, LANES), F32),
            pltpu.VMEM((3, 3, DEPTH * OUT, LANES), F32),
            pltpu.VMEM((3, 3, DEPTH, 8, LANES), F32),
            pltpu.VMEM((3, 3, DEPTH * OUT, LANES), F32),
            pltpu.VMEM((3, ROWS, DEPTH, 3 * LANES), F32),
        ],
    )(table, w, rwe, rwo, fx, sums, mask, slope, gh, gl)
    rge, rgo = swap("gx", ge, go)

    devices = lax.axis_size("gx") * ny
    local = jnp.stack([jnp.sum(loss), jnp.sum(tissue).astype(F32)])
    line = jnp.pad(local, (0, LANES - 2)).reshape(1, 1, LANES)
    everyone = lax.all_to_all(jnp.broadcast_to(line, (devices, 1, LANES)), ("gx", "gy"), 0, 0)
    totals = jnp.sum(everyone, axis=(0, 1))
    similarity_loss = -totals[0] / (totals[1] * float(BX * BY * DEPTH))

    (update,) = call(
        smooth_kernel,
        [((3, rows, 2 * LANES), F32)],
        [S] + [V] * 3,
        [A],
        [
            pltpu.VMEM((2, 3, GAUSS_RADIUS, DEPTH, 2 * LANES), F32),
            pltpu.VMEM((rows, LANES), F32),
            pltpu.VMEM((3, 2, rows, LANES), F32),
            pltpu.SemaphoreType.DMA((6,)),
        ],
    )(table, ys, rge, rgo)
    return update.reshape(velocity.shape), similarity_loss


def solution(mesh):
    in_specs = (
        P(None, "gx", "gy"),
        P(None, "gx", "gy"),
        P(None, None, "gx", "gy"),
        P(None, "gx", "gy"),
        P("gx", "gy"),
    )
    out_specs = (P(None, None, "gx", "gy"), P())
    return jax.shard_map(
        on_device, mesh=mesh, in_specs=in_specs, out_specs=out_specs, check_vma=False
    )
```

profile of v0, /device:TPU:128, one launch (start us, length us, event | category | flops | bytes accessed | tf_op | source)
XLA Modules:
  0.0 153.2 jit_solution(10365480589072174648)
XLA Ops:
  0.6 0.8 copy.11
  1.5 0.8 reshape.31
  2.9 1.8 %edge_x_kernel.1 = (bf16[272,256]{1,0:T(8,128)(2,1)}, bf16[272,256]{1,0:T(8,128)(2,1)}) custom-call(s32[20]{0:T(128)} %concatenate.3.s_ref, bf16[512,256]{1,0:T(8,128)(2,1)} %bitcast.17, bf16[512,256]{1,0:T(8,128)(2,1)} %bitcast.14), custom_call_target="tpu_custom_call" | custom-call | tf_op jit(solution)/shard_map/edge_x_kernel/pallas_call | solution.py:584
  4.7 1.5 collective-permute-start
  6.2 3.1 %collective-permute-start.1 = (bf16[272,256]{1,0:T(8,128)(2,1)}, bf16[272,256]{1,0:T(8,128)(2,1)S(1)}, u32[]{:S(2)}, u32[]{:S(2)}) collective-permute-start(bf16[272,256]{1,0:T(8,128)(2,1)} %get-tuple-element.20), channel_id=1, source_target_pairs={{16,32},{32,16},{48,64},{64,48},{80,96},{96,80},{112,128},{128,112... | collective-permute-start | bytes 417800 | tf_op jit(solution)/shard_map/ppermute | solution.py:553
  9.3 2.5 %edge_v_kernel.1 = (bf16[384,128]{1,0:T(8,128)(2,1)}, bf16[384,128]{1,0:T(8,128)(2,1)}) custom-call(s32[20]{0:T(128)} %concatenate.3.s_ref, f32[3,512,256]{2,1,0:T(8,128)} %bitcast.12), custom_call_target="tpu_custom_call" | custom-call | tf_op jit(solution)/shard_map/edge_v_kernel/pallas_call | solution.py:587
  11.9 8.7 %collective-permute-done.1.xo_ref = bf16[272,256]{1,0:T(8,128)(2,1)S(1)} collective-permute-done((bf16[272,256]{1,0:T(8,128)(2,1)}, bf16[272,256]{1,0:T(8,128)(2,1)S(1)}, u32[]{:S(2)}, u32[]{:S(2)}) %collective-permute-start.1) | collective-permute-done | bytes 139296 | tf_op jit(solution)/shard_map/ppermute | solution.py:553
  21.2 2.2 %edge_y_kernel.1 = (bf16[688,128]{1,0:T(8,128)(2,1)}, bf16[688,128]{1,0:T(8,128)(2,1)}) custom-call(s32[20]{0:T(128)} %concatenate.3.s_ref, bf16[512,256]{1,0:T(8,128)(2,1)} %bitcast.18, bf16[512,256]{1,0:T(8,128)(2,1)} %bitcast.15, bf16[272,256]{1,0:T(8,128)(2,1)} %copy-done, bf16[272,256]{1,0:T(8,128)(2,1)} %copy-done.1, ...), custom_call_target="tpu_custom_call" | custom-call | tf_op jit(solution)/shard_map/edge_y_kernel/pallas_call | solution.py:589
  24.1 1.0 collective-permute-done.2.ye_ref
  25.0 0.7 copy-done.2
  26.4 20.6 %warp_kernel.1 = (bf16[32,16,384]{2,1,0:T(8,128)(2,1)}, f32[3,32,16,384]{3,2,1,0:T(8,128)}, bf16[8,16,384]{2,1,0:T(8,128)(2,1)}, bf16[8,16,384]{2,1,0:T(8,128)(2,1)}) custom-call(s32[20]{0:T(128)} %concatenate.3.s_ref, bf16[512,256]{1,0:T(8,128)(2,1)} %bitcast.19, bf16[272,256]{1,0:T(8,128)(2,1)} %copy-done, bf16[272,256]{1,0:T(8,128)(2,1)} %copy-done.1, ...), custom_call_target="tpu_custom_call" | custom-call | tf_op jit(solution)/shard_map/warp_kernel/pallas_call | solution.py:593
  47.1 3.2 %collective-permute-start.5 = (bf16[8,16,384]{2,1,0:T(8,128)(2,1)}, bf16[8,16,384]{2,1,0:T(8,128)(2,1)S(1)}, u32[]{:S(2)}, u32[]{:S(2)}) collective-permute-start(bf16[8,16,384]{2,1,0:T(8,128)(2,1)} %get-tuple-element.27), channel_id=1, source_target_pairs={{16,32},{32,16},{48,64},{64,48},{80,96},{96,80},{112,128},{128,112... | collective-permute-start | bytes 294920 | tf_op jit(solution)/shard_map/ppermute | solution.py:553
  51.6 16.8 %fixed_kernel.1 = (bf16[48,3,16,128]{3,2,1,0:T(8,128)(2,1)}, f32[2,3,640,128]{3,2,1,0:T(8,128)}, f32[3,40,128]{2,1,0:T(8,128)}) custom-call(s32[20]{0:T(128)} %concatenate.3.s_ref, bf16[512,256]{1,0:T(8,128)(2,1)} %bitcast.16, bf16[272,256]{1,0:T(8,128)(2,1)} %copy-done, bf16[272,256]{1,0:T(8,128)(2,1)} %copy-done.1, bf16[688,128]{1,0:T(8,128)(2,1)} %copy-done.2, ...), custom_call_target="tpu_custom_call" | custom-call | tf_op jit(solution)/shard_map/fixed_kernel/pallas_call | solution.py:607
  69.1 35.0 %gradient_kernel.1 = (f32[3,32,16,256]{3,2,1,0:T(8,128)}, bf16[3,7,16,256]{3,2,1,0:T(8,128)(2,1)}, bf16[3,7,16,256]{3,2,1,0:T(8,128)(2,1)}, f32[8,128]{1,0:T(8,128)}) custom-call(s32[20]{0:T(128)} %concatenate.3.s_ref, bf16[32,16,384]{2,1,0:T(8,128)(2,1)} %get-tuple-element.25.w_ref, bf16[8,16,384]{2,1,0:T(8,128)(2,1)} %copy-done.6, ...), custom_call_target="tpu_custom_call" | custom-call | tf_op jit(solution)/shard_map/gradient_kernel/pallas_call | solution.py:621
  104.1 1.3 reduce_sum.27
  105.4 0.7 fusion
  106.1 0.7 broadcast_in_dim.2
  106.8 19.7 %all-to-all-start = ((f32[256,1,128]{2,1,0:T(1,128)}), f32[256,1,128]{2,1,0:T(1,128)S(1)}, u32[]{:S(2)}, u32[]{:S(2)}) async-start(f32[256,1,128]{2,1,0:T(1,128)} %broadcast_in_dim.2), calls=%async_computation | async-start | bytes 262144 | tf_op jit(solution)/shard_map/all_to_all | solution.py:639
  126.6 1.6 %collective-permute-start.6 = (bf16[3,7,16,256]{3,2,1,0:T(8,128)(2,1)}, bf16[3,7,16,256]{3,2,1,0:T(8,128)(2,1)S(1)}, u32[]{:S(2)}, u32[]{:S(2)}) collective-permute-start(bf16[3,7,16,256]{3,2,1,0:T(8,128)(2,1)} %get-tuple-element.33), channel_id=1, source_target_pairs={{0,16},{16,0},{32,48},{48,32},{64,80},{80,64},{96,112},{112,96},{1... | collective-permute-start | bytes 516104 | tf_op jit(solution)/shard_map/ppermute | solution.py:553
  128.1 3.4 %collective-permute-start.7 = (bf16[3,7,16,256]{3,2,1,0:T(8,128)(2,1)}, bf16[3,7,16,256]{3,2,1,0:T(8,128)(2,1)S(1)}, u32[]{:S(2)}, u32[]{:S(2)}) collective-permute-start(bf16[3,7,16,256]{3,2,1,0:T(8,128)(2,1)} %get-tuple-element.34), channel_id=1, source_target_pairs={{16,32},{32,16},{48,64},{64,48},{80,96},{96,80},{112,128},{128,112... | collective-permute-start | bytes 516104 | tf_op jit(solution)/shard_map/ppermute | solution.py:553
  131.6 2.0 %collective-permute-done.6.ge_ref = bf16[3,7,16,256]{3,2,1,0:T(8,128)(2,1)S(1)} collective-permute-done((bf16[3,7,16,256]{3,2,1,0:T(8,128)(2,1)}, bf16[3,7,16,256]{3,2,1,0:T(8,128)(2,1)S(1)}, u32[]{:S(2)}, u32[]{:S(2)}) %collective-permute-start.6) | collective-permute-done | bytes 172064 | tf_op jit(solution)/shard_map/ppermute | solution.py:553
  133.5 10.7 %collective-permute-done.7.go_ref = bf16[3,7,16,256]{3,2,1,0:T(8,128)(2,1)S(1)} collective-permute-done((bf16[3,7,16,256]{3,2,1,0:T(8,128)(2,1)}, bf16[3,7,16,256]{3,2,1,0:T(8,128)(2,1)S(1)}, u32[]{:S(2)}, u32[]{:S(2)}) %collective-permute-start.7) | collective-permute-done | bytes 172064 | tf_op jit(solution)/shard_map/ppermute | solution.py:553
  144.2 0.7 copy-done.5
  144.9 5.3 %smooth_kernel.1 = f32[3,512,256]{2,1,0:T(8,128)} custom-call(s32[20]{0:T(128)} %concatenate.3.s_ref, f32[3,32,16,256]{3,2,1,0:T(8,128)} %get-tuple-element.32.ys_ref, bf16[3,7,16,256]{3,2,1,0:T(8,128)(2,1)} %copy-done.4, bf16[3,7,16,256]{3,2,1,0:T(8,128)(2,1)} %copy-done.5), custom_call_target="tpu_custom_call" | custom-call | tf_op jit(solution)/shard_map/smooth_kernel/pallas_call | solution.py:643
  (29 shorter events, 4.8 us)
Async XLA Ops:
  4.7 7.1 %collective-permute-start = (bf16[272,256]{1,0:T(8,128)(2,1)}, bf16[272,256]{1,0:T(8,128)(2,1)S(1)}, u32[]{:S(2)}, u32[]{:S(2)}) collective-permute-start(bf16[272,256]{1,0:T(8,128)(2,1)} %get-tuple-element.19), channel_id=1, source_target_pairs={{0,16},{16,0},{32,48},{48,32},{64,80},{80,64},{96,112},{112,96},{1... | collective-permute-start | bytes 417800 | tf_op jit(solution)/shard_map/ppermute | solution.py:553
  6.2 14.3 %collective-permute-start.1 = (bf16[272,256]{1,0:T(8,128)(2,1)}, bf16[272,256]{1,0:T(8,128)(2,1)S(1)}, u32[]{:S(2)}, u32[]{:S(2)}) collective-permute-start(bf16[272,256]{1,0:T(8,128)(2,1)} %get-tuple-element.20), channel_id=1, source_target_pairs={{16,32},{32,16},{48,64},{64,48},{80,96},{96,80},{112,128},{128,112... | collective-permute-start | bytes 417800 | tf_op jit(solution)/shard_map/ppermute | solution.py:553
  11.9 8.7 %copy-start = (bf16[272,256]{1,0:T(8,128)(2,1)}, bf16[272,256]{1,0:T(8,128)(2,1)S(1)}, u32[]{:S(2)}) copy-start(bf16[272,256]{1,0:T(8,128)(2,1)S(1)} %collective-permute-done.xe_ref) | copy-start | bytes 417796
  20.6 0.7 copy-start.1
  21.2 29.1 %copy-start.8 = (s32[2,2]{1,0:T(2,128)S(1)}, s32[2,2]{1,0:T(2,128)}, u32[]{:S(2)}) copy-start(s32[2,2]{1,0:T(2,128)} %param.10) | copy-start | bytes 52
  23.4 1.6 %collective-permute-start.2 = (bf16[688,128]{1,0:T(8,128)(2,1)}, bf16[688,128]{1,0:T(8,128)(2,1)S(1)}, u32[]{:S(2)}, u32[]{:S(2)}) collective-permute-start(bf16[688,128]{1,0:T(8,128)(2,1)} %get-tuple-element.23), channel_id=1, source_target_pairs={{0,1},{1,0},{2,3},{3,2},{4,5},{5,4},{6,7},{7,6},{8,9},{9,8},{10,11... | collective-permute-start | bytes 528392 | tf_op jit(solution)/shard_map/ppermute | solution.py:553
  23.4 1.6 %collective-permute-start.3 = (bf16[688,128]{1,0:T(8,128)(2,1)}, bf16[688,128]{1,0:T(8,128)(2,1)S(1)}, u32[]{:S(2)}, u32[]{:S(2)}) collective-permute-start(bf16[688,128]{1,0:T(8,128)(2,1)} %get-tuple-element.24), channel_id=1, source_target_pairs={{1,2},{2,1},{3,4},{4,3},{5,6},{6,5},{7,8},{8,7},{9,10},{10,9},{11,... | collective-permute-start | bytes 528392 | tf_op jit(solution)/shard_map/ppermute | solution.py:553
  25.0 0.7 copy-start.2
  25.7 0.7 copy-start.3
  47.0 21.4 %collective-permute-start.4 = (bf16[8,16,384]{2,1,0:T(8,128)(2,1)}, bf16[8,16,384]{2,1,0:T(8,128)(2,1)S(1)}, u32[]{:S(2)}, u32[]{:S(2)}) collective-permute-start(bf16[8,16,384]{2,1,0:T(8,128)(2,1)} %get-tuple-element.26), channel_id=1, source_target_pairs={{0,16},{16,0},{32,48},{48,32},{64,80},{80,64},{96,112},{112,96},{1... | collective-permute-start | bytes 294920 | tf_op jit(solution)/shard_map/ppermute | solution.py:553
  47.1 21.3 %collective-permute-start.5 = (bf16[8,16,384]{2,1,0:T(8,128)(2,1)}, bf16[8,16,384]{2,1,0:T(8,128)(2,1)S(1)}, u32[]{:S(2)}, u32[]{:S(2)}) collective-permute-start(bf16[8,16,384]{2,1,0:T(8,128)(2,1)} %get-tuple-element.27), channel_id=1, source_target_pairs={{16,32},{32,16},{48,64},{64,48},{80,96},{96,80},{112,128},{128,112... | collective-permute-start | bytes 294920 | tf_op jit(solution)/shard_map/ppermute | solution.py:553
  68.4 0.6 copy-start.6
  68.4 0.7 copy-start.7
  106.8 43.4 %all-to-all-start = ((f32[256,1,128]{2,1,0:T(1,128)}), f32[256,1,128]{2,1,0:T(1,128)S(1)}, u32[]{:S(2)}, u32[]{:S(2)}) async-start(f32[256,1,128]{2,1,0:T(1,128)} %broadcast_in_dim.2), calls=%async_computation | async-start | bytes 262144 | tf_op jit(solution)/shard_map/all_to_all | solution.py:639
  126.6 7.0 %collective-permute-start.6 = (bf16[3,7,16,256]{3,2,1,0:T(8,128)(2,1)}, bf16[3,7,16,256]{3,2,1,0:T(8,128)(2,1)S(1)}, u32[]{:S(2)}, u32[]{:S(2)}) collective-permute-start(bf16[3,7,16,256]{3,2,1,0:T(8,128)(2,1)} %get-tuple-element.33), channel_id=1, source_target_pairs={{0,16},{16,0},{32,48},{48,32},{64,80},{80,64},{96,112},{112,96},{1... | collective-permute-start | bytes 516104 | tf_op jit(solution)/shard_map/ppermute | solution.py:553
  128.1 16.1 %collective-permute-start.7 = (bf16[3,7,16,256]{3,2,1,0:T(8,128)(2,1)}, bf16[3,7,16,256]{3,2,1,0:T(8,128)(2,1)S(1)}, u32[]{:S(2)}, u32[]{:S(2)}) collective-permute-start(bf16[3,7,16,256]{3,2,1,0:T(8,128)(2,1)} %get-tuple-element.34), channel_id=1, source_target_pairs={{16,32},{32,16},{48,64},{64,48},{80,96},{96,80},{112,128},{128,112... | collective-permute-start | bytes 516104 | tf_op jit(solution)/shard_map/ppermute | solution.py:553
  133.5 10.7 %copy-start.4 = (bf16[3,7,16,256]{3,2,1,0:T(8,128)(2,1)}, bf16[3,7,16,256]{3,2,1,0:T(8,128)(2,1)S(1)}, u32[]{:S(2)}) copy-start(bf16[3,7,16,256]{3,2,1,0:T(8,128)(2,1)S(1)} %collective-permute-done.6.ge_ref) | copy-start | bytes 516100
  144.2 0.7 copy-start.5
where the time goes:
time: 154 us; the launch traced here: 153 us
  Pallas kernels  84.3 us (55%)
  starting transfers between devices  33.3 us (22%)
  waiting for transfers between devices  22.3 us (14%)
  local copies, waits for them, and re-layouts  6.93 us (4%)
  between operations  3.77 us (2%)
  other arithmetic  2.68 us (2%)
    pallas_call x1, Pallas kernels, on_device(): call(gradient_kernel, [((3, ROWS, DEPTH, 2 * LANES), F32), edge, edge, ((...  35 us
    ppermute x8, waiting for transfers between devices, swap(): return (lax.ppermute(even, axis, first), lax.ppermute(odd, axis, second))  22.3 us
    pallas_call x1, Pallas kernels, on_device(): call(warp_kernel, [((ROWS, DEPTH, 3 * LANES), BF16), ((3, ROWS, DEPTH, 3...  20.6 us
    all_to_all x1, starting transfers between devices, on_device(): lax.all_to_all(jnp.broadcast_to(line, (devices, 1, LANES)), ('gx', 'gy'),...  19.7 us
    pallas_call x1, Pallas kernels, on_device(): call(fixed_kernel, [((EXT, 3, DEPTH, LANES), BF16), ((2, 3, DEPTH * OUT,...  16.8 us
    ppermute x8, starting transfers between devices, swap(): return (lax.ppermute(even, axis, first), lax.ppermute(odd, axis, second))  13.5 us
    pallas_call x1, Pallas kernels, on_device(): call(smooth_kernel, [((3, rows, 2 * LANES), F32)], [S] + [V] * 3, [A], [p...  5.32 us
    unnamed x19, local copies, waits for them, and re-layouts  4.11 us
  transfers between devices with their start and end apart: 9, of which 4 were waited for; matrix products, arithmetic and copies ran while one was open for 0% of the time, Pallas kernels for 16%

commit v1 on v0

--- a/solution.py
+++ b/solution.py
@@ -17,6 +17,7 @@
 OUT = 40
 LANES = 128
 GAUSS_RADIUS = 7
+BOX_RADIUS = 4
 GAUSS_SIGMA = 3.0
 WINDOW_COUNT = 729.0
 VAR_EPSILON = 1e-05
@@ -38,6 +39,14 @@
     ]
     total = sum(raw)
     return [w / total for w in raw]
+
+
+def unrolled(count):
+    def run(body):
+        for i in range(count):
+            body(i)
+
+    return run
 
 
 def lane_iota(shape):
@@ -195,13 +204,15 @@
         left = left[:64] + left[64:]
         for k in range(8):
             v_scr[c, 2, 64 * k : 64 * k + 64] = unpack_group(right, left, k, 8)
-    m_right, m_left = sides_of(py, ye_ref, yo_ref, Y_META, 16)
-    lane8 = lane_iota((16, LANES))
-    first_row = lax.broadcasted_iota(jnp.int32, (16, LANES), 0) == 0
-
-    def scalar(meta, k):
-        return jnp.sum(jnp.where(first_row & (lane8 == k), meta, 0.0)).astype(jnp.int32)
-
+    digit = lax.broadcasted_iota(jnp.int32, (16, LANES), 1)
+    power = (1 << (4 * jnp.minimum(digit, 5))).astype(F32)
+    use = (lax.broadcasted_iota(jnp.int32, (16, LANES), 0) == 0) & (digit < 6)
+
+    def offsets_of(meta):
+        code = jnp.sum(jnp.where(use, (meta + 8.0) * power, 0.0)).astype(jnp.int32)
+        return [((code >> (4 * k)) & 15) - 8 for k in range(6)]
+
+    m_right, m_left = (offsets_of(x) for x in sides_of(py, ye_ref, yo_ref, Y_META, 16))
     lane = lane_iota((DEPTH, LANES))
 
     def gather(j, xb, oz, ox, oy, merge):
@@ -215,7 +226,7 @@
             shifts.append((nbr, mask, (LANES - s) & (LANES - 1)))
         base = (3 + oz) * EXT + xb * BX + 8 + ox
 
-        @pl.loop(0, BX + 1)
+        @unrolled(BX + 1)
         def _(x):
             for c in range(2):
                 start = base + c * EXT + x
@@ -229,7 +240,7 @@
                     r_scr[b, c, x] = val
 
     def blend(j, xb):
-        @pl.loop(0, BX)
+        @pl.loop(0, BX, unroll=4)
         def _(x):
             row = xb * BX + x
             f0, f1, f2 = (v_scr[c, j, pl.ds(row, DEPTH, stride=ROWS), :] for c in range(3))
@@ -253,8 +264,8 @@
             slope_ref[2, row, :, lanes] = dy[0] + f0 * (dy[1] - dy[0])
 
     for xb in range(2):
-        gather(2, xb, *(scalar(m_right, 2 * c + xb) for c in range(3)), False)
-        gather(2, xb, *(scalar(m_left, 2 * c + xb) for c in range(3)), True)
+        gather(2, xb, *(m_right[2 * c + xb] for c in range(3)), False)
+        gather(2, xb, *(m_left[2 * c + xb] for c in range(3)), True)
         blend(2, xb)
     for copy in copies:
         copy.wait()
@@ -291,24 +302,42 @@
     return [add_all([three[z - 3], three[z], three[z + 3]]) for z in range(DEPTH)]
 
 
-def shift_y(v, s):
-    lane = lane_iota(v[0].shape)
-    if s > 0:
-        return [roll(jnp.where(lane < s, v[(j + 1) % 3], v[j]), -s) for j in range(3)]
-    return [roll(jnp.where(lane >= LANES + s, v[(j + 2) % 3], v[j]), -s) for j in range(3)]
-
-
-def box_y(v):
-    for s in (1, 3):
-        a, b = shift_y(v, s), shift_y(v, -s)
-        v = [x + y + z for x, y, z in zip(a, v, b)]
-    return v
-
-
-def fixed_kernel(
-    s_ref, f_ref, xe_ref, xo_ref, ye_ref, yo_ref,
-    fx_ref, sum_ref, mask_ref,
-    f_scr, z_scr, b_scr,
+def split(v):
+    hi = v.astype(BF16)
+    return hi, (v - hi.astype(F32)).astype(BF16)
+
+
+def dot(a, b):
+    return jnp.dot(a, b, preferred_element_type=F32)
+
+
+def box_y(parts, band):
+    total = None
+    for p in parts:
+        d = dot(p, band)
+        total = d if total is None else total + d
+    return total
+
+
+def put_tiles(ref, q, first, v):
+    for j in range(3):
+        ref[q, j, pl.ds(first, v.shape[0]), :] = v[:, LANES * j : LANES * j + LANES]
+
+
+def box_z_in_place(ref, q, count):
+    @pl.loop(0, count // 8)
+    def _(t):
+        for j in range(3):
+            rows = [pl.ds(t * 128 + z, 8, stride=DEPTH) for z in range(DEPTH)]
+            v = box_z([ref[q, j, r, :] for r in rows])
+            for z in range(DEPTH):
+                ref[q, j, rows[z], :] = v[z]
+
+
+def window_kernel(
+    s_ref, f_ref, xe_ref, xo_ref, ye_ref, yo_ref, w_ref, band_ref,
+    fx_ref, sum_ref, mask_ref, own_ref,
+    f_scr, y_scr,
 ):
     px = s_ref[PX]
     py = s_ref[PY]
@@ -342,144 +371,154 @@
             t = [jnp.where(half, column(m_right, k), column(m_left, k)) for k in range(4)]
         mask_ref[j] = jnp.where(row < 4, t[0], jnp.where(row < 20, t[1], jnp.where(row < 36, t[2], t[3])))
 
-    @pl.loop(0, 3)
-    def _(j):
-        def load(x):
-            return f_scr[j, pl.ds(x, DEPTH, stride=EXT), :]
-
-        for q in range(2):
-            def value(x):
-                v = load(x)
-                if q == 0:
-                    fx_ref[x, j] = v.astype(BF16)
-                return v if q == 0 else v * v
+    for x in range(EXT):
+        for j in range(3):
+            v = f_scr[j, pl.ds(x, DEPTH, stride=EXT), :]
+            fx_ref[x, :, LANES * j : LANES * j + LANES] = v.astype(BF16)
+
+    band = band_ref[...]
+    for part in range(3):
+        x = 16 * part
+        f = fx_ref[x : x + 16].reshape(256, 3 * LANES)
+        v = f.astype(F32)
+        put_tiles(y_scr, 0, 256 * part, box_y([f], band))
+        put_tiles(y_scr, 1, 256 * part, box_y(split(v * v), band))
+    for part in range(2):
+        x = 16 * part
+        w = w_ref[x : x + 16].reshape(256, 3 * LANES)
+        f = fx_ref[x + 8 : x + 24].reshape(256, 3 * LANES)
+        image_sums(own_ref, 256 * part, w, f, band)
+    for q in range(2):
+        box_z_in_place(y_scr, q, EXT)
+        for j in range(3):
+            def load(x):
+                return y_scr[q, j, DEPTH * x : DEPTH * x + DEPTH]
 
             def store(x, v):
-                z_scr[q, j, pl.ds(x, DEPTH, stride=OUT), :] = v
-
-            box_x(value, store, OUT)
-
-    sum_zy(z_scr, b_scr, 2, lambda z, at, sums: put_sums(sum_ref, at, sums))
-
-
-def put_sums(ref, at, sums):
-    for q, v in enumerate(sums):
-        for j in range(3):
-            ref[q, j, pl.ds(at, 8), :] = v[j]
-
-
-def sum_zy(z_scr, b_scr, count, use):
-    @pl.loop(0, OUT // 8)
-    def _(t):
-        def at(z):
-            return pl.multiple_of(z * OUT + t * 8, 8)
-
-        for q in range(count):
-            for j in range(3):
-                v = box_z([z_scr[q, j, pl.ds(at(z), 8), :] for z in range(DEPTH)])
-                for z in range(DEPTH):
-                    b_scr[q, j, z] = v[z]
-
-        @pl.loop(0, DEPTH)
-        def _(z):
-            use(t, at(z), [box_y([b_scr[q, j, z] for j in range(3)]) for q in range(count)])
+                sum_ref[q, j, DEPTH * x : DEPTH * x + DEPTH] = v
+
+            box_x(load, store, OUT)
+    for q in range(3):
+        box_z_in_place(own_ref, q, ROWS)
+
+
+def image_sums(ref, first, w, f, band):
+    i = w.astype(F32)
+    put_tiles(ref, 0, first, box_y([w], band))
+    put_tiles(ref, 1, first, box_y(split(i * i), band))
+    put_tiles(ref, 2, first, box_y(split(i * f.astype(F32)), band))
 
 
 def gradient_kernel(
-    s_ref, w_ref, we_ref, wo_ref, fx_ref, sum_ref, mask_ref, slope_ref, gh_ref, gl_ref,
+    s_ref, w_ref, we_ref, wo_ref, fx_ref, sum_ref, mask_ref, own_ref, slope_ref,
+    band_ref, gh_ref, gl_ref,
     ys_ref, e_ref, o_ref, loss_ref,
-    i_scr, z_scr, b_scr, a_scr, g_scr,
+    h_scr, s_scr, a_scr, b_scr,
 ):
     px = s_ref[PX]
+    band = band_ref[...]
     before, after = before_after(px, we_ref[...].astype(F32), wo_ref[...].astype(F32))
-    for j in range(3):
-        lanes = slice(LANES * j, LANES * j + LANES)
-        i_scr[0:8, j] = before[:, :, lanes]
-        i_scr[8:40, j] = w_ref[:, :, lanes].astype(F32)
-        i_scr[40:48, j] = after[:, :, lanes]
+    w = jnp.concatenate([before, after], axis=0).astype(BF16).reshape(256, 3 * LANES)
+    f = jnp.concatenate([fx_ref[0:8], fx_ref[40:48]], axis=0).reshape(256, 3 * LANES)
+    image_sums(h_scr, 0, w, f, band)
+    for q in range(3):
+        box_z_in_place(h_scr, q, 16)
 
     @pl.loop(0, 3)
     def _(j):
         for q in range(3):
-            def value(x):
-                v = i_scr[x, j]
-                if q == 0:
-                    return v
-                return v * (v if q == 1 else fx_ref[x, j].astype(F32))
+            def load(x):
+                if 8 <= x < 40:
+                    return own_ref[q, j, DEPTH * (x - 8) : DEPTH * (x - 7)]
+                x = x if x < 8 else x - 32
+                return h_scr[q, j, DEPTH * x : DEPTH * x + DEPTH]
 
             def store(x, v):
-                z_scr[q, j, pl.ds(x, DEPTH, stride=OUT), :] = v
-
-            box_x(value, store, OUT)
-
-    loss_ref[...] = jnp.zeros((8, LANES), F32)
-    rows8 = lax.broadcasted_iota(jnp.int32, (8, LANES), 0)
-
-    def stats(t, at, sums):
-        inner = (rows8 + t * 8 >= 4) & (rows8 + t * 8 < 4 + ROWS)
+                s_scr[q, j, DEPTH * x : DEPTH * x + DEPTH] = v
+
+            box_x(load, store, OUT)
+
+    lane = lane_iota((DEPTH, LANES))
+    near = (lane < 11) | (lane >= LANES - 11)
+
+    def stats(x, inner):
         total = None
+        first = x * DEPTH
+        rows = pl.ds(pl.multiple_of(first, DEPTH) if inner else first, DEPTH)
         for j in range(3):
-            si, sii, sij = (sums[q][j] for q in range(3))
-            sj = sum_ref[0, j, pl.ds(at, 8), :]
-            sjj = sum_ref[1, j, pl.ds(at, 8), :]
-            m = mask_ref[j, pl.ds(pl.multiple_of(t * 8, 8), 8), :]
+            si, sii, sij = (s_scr[q, j, rows, :] for q in range(3))
+            sj = sum_ref[0, j, rows, :]
+            sjj = sum_ref[1, j, rows, :]
+            m = jnp.broadcast_to(mask_ref[j, pl.ds(x, 1), :], (DEPTH, LANES))
             cross = sij - si * sj * (1.0 / WINDOW_COUNT)
             var_i = sii - si * si * (1.0 / WINDOW_COUNT)
             var_j = sjj - sj * sj * (1.0 / WINDOW_COUNT)
             quotient = cross / (var_i * var_j + VAR_EPSILON)
             second = quotient * quotient * var_j
-            a_scr[0, j, pl.ds(at, 8), :] = (2.0 / WINDOW_COUNT) * m * (quotient * sj - second * si)
-            a_scr[1, j, pl.ds(at, 8), :] = m * second
-            a_scr[2, j, pl.ds(at, 8), :] = -2.0 * m * quotient
-            if j < 2:
-                ncc = jnp.where(inner, m * (cross * quotient), 0.0)
+            adjoint = (
+                (2.0 / WINDOW_COUNT) * m * (quotient * sj - second * si),
+                m * second,
+                -2.0 * m * quotient,
+            )
+            for k in range(3):
+                a_scr[k, j, rows, :] = adjoint[k] if j < 2 else jnp.where(near, adjoint[k], 0.0)
+            if inner and j < 2:
+                ncc = m * (cross * quotient)
                 total = ncc if total is None else total + ncc
-        loss_ref[...] += total
-
-    sum_zy(z_scr, b_scr, 3, stats)
-    sum_zy(a_scr, b_scr, 3, lambda t, at, sums: put_sums(z_scr, at, sums))
-
-    lane = lane_iota((DEPTH, LANES))
-    has_r = s_ref[HAS_R]
-    has_l = s_ref[HAS_L]
-    r_lim = jnp.where(has_r == 1, GAUSS_RADIUS, 0)
-    l_lim = jnp.where(has_l == 1, LANES - GAUSS_RADIUS, LANES)
-    valid = (lane < r_lim) | (lane >= l_lim)
+        if inner:
+            loss_ref[...] += total
+
+    loss_ref[...] = jnp.zeros((DEPTH, LANES), F32)
+
+    @pl.loop(0, ROWS, unroll=2)
+    def _(x):
+        stats(x + 4, True)
+
+    for x in (0, 1, 2, 3, 36, 37, 38, 39):
+        stats(x, False)
+
+    for k in range(3):
+        box_z_in_place(a_scr, k, OUT)
 
     for j in range(3):
         lanes = slice(LANES * j, LANES * j + LANES)
-        for q in range(3):
+        for k in range(3):
             def load(x):
-                return z_scr[q, j, pl.ds(x, DEPTH, stride=OUT), :]
+                return a_scr[k, j, DEPTH * x : DEPTH * x + DEPTH]
 
             def store(x, v):
-                if q == 0:
-                    g_scr[0, x, :, lanes] = v
-                elif q == 1:
-                    g_scr[0, x, :, lanes] += 2.0 * i_scr[x + 8, j] * v
-                else:
-                    grad = g_scr[0, x, :, lanes] + fx_ref[x + 8, j].astype(F32) * v
-                    for c in (2, 1, 0):
-                        val = grad * slope_ref[c, x, :, lanes]
-                        if j == 2:
-                            val = jnp.where(valid, val, 0.0)
-                        g_scr[c, x, :, lanes] = val
+                hi, lo = split(v)
+                b_scr[k, 0, x, :, lanes] = hi
+                b_scr[k, 1, x, :, lanes] = lo
 
             box_x(load, store, ROWS)
 
+    column = lane_iota((1, 3 * LANES))
+    r_lim = jnp.where(s_ref[HAS_R] == 1, 2 * LANES + GAUSS_RADIUS, 2 * LANES)
+    l_lim = jnp.where(s_ref[HAS_L] == 1, 3 * LANES - GAUSS_RADIUS, 3 * LANES)
+    valid = (column < r_lim) | (column >= l_lim)
     gh = gh_ref[...]
     gl = gl_ref[...]
+    for part in range(2):
+        x = 16 * part
+
+        def flat(v):
+            return v.reshape(256, 3 * LANES)
+
+        spread = [
+            box_y([flat(b_scr[k, i, x : x + 16]) for i in range(2)], band) for k in range(3)
+        ]
+        i = flat(w_ref[x : x + 16]).astype(F32)
+        t = flat(fx_ref[x + 8 : x + 24]).astype(F32)
+        grad = spread[0] + 2.0 * i * spread[1] + t * spread[2]
+        for c in range(3):
+            g = jnp.where(valid, grad * flat(slope_ref[c, x : x + 16]), 0.0)
+            hi, lo = split(g)
+            ys = dot(hi, gh) + dot(lo, gh) + dot(hi, gl)
+            ys_ref[c, x : x + 16] = ys.reshape(16, DEPTH, 2 * LANES)
     for c in range(3):
-        g = g_scr[c].reshape(ROWS * DEPTH, 3 * LANES)
-        hi = g.astype(BF16)
-        lo = (g - hi.astype(F32)).astype(BF16)
-        ys = jnp.dot(hi, gh, preferred_element_type=F32)
-        ys = ys + jnp.dot(lo, gh, preferred_element_type=F32)
-        ys = ys + jnp.dot(hi, gl, preferred_element_type=F32)
-        ys = ys.reshape(ROWS, DEPTH, 2 * LANES)
-        ys_ref[c] = ys
-        first = ys[:GAUSS_RADIUS]
-        last = ys[ROWS - GAUSS_RADIUS :]
+        first = ys_ref[c, :GAUSS_RADIUS]
+        last = ys_ref[c, ROWS - GAUSS_RADIUS :]
         e_ref[c] = pick(px, last, first).astype(BF16)
         o_ref[c] = pick(px, first, last).astype(BF16)
 
@@ -553,15 +592,19 @@
     return lax.ppermute(even, axis, first), lax.ppermute(odd, axis, second)
 
 
-def gauss_matrices():
+def matrices():
     weights = gauss_weights()
-    g = np.zeros((3 * LANES, 2 * LANES), np.float32)
-    for col in range(2 * LANES):
+    size = 3 * LANES
+    g = np.zeros((size, 2 * LANES), np.float32)
+    band = np.zeros((size, size), np.float32)
+    for col in range(size):
         for tap in range(-GAUSS_RADIUS, GAUSS_RADIUS + 1):
-            g[(col + tap) % (3 * LANES), col] = weights[tap + GAUSS_RADIUS]
-    hi = jnp.asarray(g).astype(BF16)
-    lo = (jnp.asarray(g) - hi.astype(F32)).astype(BF16)
-    return hi, lo
+            if col < 2 * LANES:
+                g[(col + tap) % size, col] = weights[tap + GAUSS_RADIUS]
+            if abs(tap) <= BOX_RADIUS:
+                band[(col + tap) % size, col] = 1.0
+    hi, lo = split(jnp.asarray(g))
+    return hi, lo, jnp.asarray(band).astype(BF16)
 
 
 def on_device(moving_image, fixed_image, velocity, offsets, tissue):
@@ -604,33 +647,34 @@
     )(table, m, rxe, rxo, rye, ryo, v)
     rwe, rwo = swap("gx", we, wo)
 
-    fx, sums, mask = call(
-        fixed_kernel,
-        [((EXT, 3, DEPTH, LANES), BF16), ((2, 3, DEPTH * OUT, LANES), F32), ((3, OUT, LANES), F32)],
-        [S] + [V] * 5,
-        [V] * 3,
+    gh, gl, band = matrices()
+    rows3 = (3, 3, rows, LANES)
+    fx, sums, mask, own = call(
+        window_kernel,
         [
-            pltpu.VMEM((3, DEPTH * EXT, LANES), F32),
-            pltpu.VMEM((2, 3, DEPTH * OUT, LANES), F32),
-            pltpu.VMEM((2, 3, DEPTH, 8, LANES), F32),
+            ((EXT, DEPTH, 3 * LANES), BF16),
+            ((2, 3, DEPTH * OUT, LANES), F32),
+            ((3, OUT, LANES), F32),
+            (rows3, F32),
         ],
-    )(table, f, rxe, rxo, rye, ryo)
-
-    gh, gl = gauss_matrices()
+        [S] + [V] * 7,
+        [V] * 4,
+        [pltpu.VMEM((3, DEPTH * EXT, LANES), F32), pltpu.VMEM((2, 3, DEPTH * EXT, LANES), F32)],
+    )(table, f, rxe, rxo, rye, ryo, w, band)
+
     edge = ((3, GAUSS_RADIUS, DEPTH, 2 * LANES), BF16)
     ys, ge, go, loss = call(
         gradient_kernel,
-        [((3, ROWS, DEPTH, 2 * LANES), F32), edge, edge, ((8, LANES), F32)],
-        [S] + [V] * 9,
+        [((3, ROWS, DEPTH, 2 * LANES), F32), edge, edge, ((DEPTH, LANES), F32)],
+        [S] + [V] * 11,
         [V] * 4,
         [
-            pltpu.VMEM((EXT, 3, DEPTH, LANES), F32),
+            pltpu.VMEM((3, 3, 256, LANES), F32),
             pltpu.VMEM((3, 3, DEPTH * OUT, LANES), F32),
-            pltpu.VMEM((3, 3, DEPTH, 8, LANES), F32),
             pltpu.VMEM((3, 3, DEPTH * OUT, LANES), F32),
-            pltpu.VMEM((3, ROWS, DEPTH, 3 * LANES), F32),
+            pltpu.VMEM((3, 2, ROWS, DEPTH, 3 * LANES), BF16),
         ],
-    )(table, w, rwe, rwo, fx, sums, mask, slope, gh, gl)
+    )(table, w, rwe, rwo, fx, sums, mask, own, slope, band, gh, gl)
     rge, rgo = swap("gx", ge, go)
 
     devices = lax.axis_size("gx") * ny

time: 154 us -> 112 us (0.73)
  Pallas kernels: 84.3 us -> 42 us
    pallas_call x1, Pallas kernels: 35 us -> 12.7 us  [on_device(): call(gradient_kernel, [((3, ROWS, DEPTH, 2 * LANES), F32), edge, edge, ((...]
    pallas_call x1, Pallas kernels: 20.6 us -> 8.22 us  [on_device(): call(warp_kernel, [((ROWS, DEPTH, 3 * LANES), BF16), ((3, ROWS, DEPTH, 3...]
    pallas_call x1, Pallas kernels: 16.8 us -> 9.22 us  [on_device(): call(window_kernel, [((EXT, DEPTH, 3 * LANES), BF16), ((2, 3, DEPTH * OUT...]
  transfers between devices with their start and end apart: 9 -> 9, of which waited for: 4 -> 4; matrix products, arithmetic and copies ran while one was open for 0% -> 1% of each run, Pallas kernels for 16% -> 15%
where the time goes in v1:
time: 112 us; the launch traced here: 111 us
  Pallas kernels  42 us (38%)
  starting transfers between devices  33.5 us (30%)
  waiting for transfers between devices  22.3 us (20%)
  local copies, waits for them, and re-layouts  6.92 us (6%)
  between operations  3.78 us (3%)
  other arithmetic  2.7 us (2%)
    ppermute x8, waiting for transfers between devices, swap(): return (lax.ppermute(even, axis, first), lax.ppermute(odd, axis, second))  22.3 us
    all_to_all x1, starting transfers between devices, on_device(): lax.all_to_all(jnp.broadcast_to(line, (devices, 1, LANES)), ('gx', 'gy'),...  19.8 us
    ppermute x8, starting transfers between devices, swap(): return (lax.ppermute(even, axis, first), lax.ppermute(odd, axis, second))  13.7 us
    pallas_call x1, Pallas kernels, on_device(): call(gradient_kernel, [((3, ROWS, DEPTH, 2 * LANES), F32), edge, edge, ((...  12.7 us
    pallas_call x1, Pallas kernels, on_device(): call(window_kernel, [((EXT, DEPTH, 3 * LANES), BF16), ((2, 3, DEPTH * OUT...  9.22 us
    pallas_call x1, Pallas kernels, on_device(): call(warp_kernel, [((ROWS, DEPTH, 3 * LANES), BF16), ((3, ROWS, DEPTH, 3...  8.22 us
    pallas_call x1, Pallas kernels, on_device(): call(smooth_kernel, [((3, rows, 2 * LANES), F32)], [S] + [V] * 3, [A], [p...  5.32 us
    unnamed x19, local copies, waits for them, and re-layouts  4.11 us
  transfers between devices with their start and end apart: 9, of which 4 were waited for; matrix products, arithmetic and copies ran while one was open for 1% of the time, Pallas kernels for 15%

profile of v1, /device:TPU:128, one launch (start us, length us, event | category | flops | bytes accessed | tf_op | source)
XLA Modules:
  0.0 111.1 jit_solution(12008301489969682061)
XLA Ops:
  0.6 0.8 copy.12
  1.5 0.8 reshape.31
  2.9 1.8 %edge_x_kernel.1 = (bf16[272,256]{1,0:T(8,128)(2,1)}, bf16[272,256]{1,0:T(8,128)(2,1)}) custom-call(s32[20]{0:T(128)} %concatenate.3.s_ref, bf16[512,256]{1,0:T(8,128)(2,1)} %bitcast.17, bf16[512,256]{1,0:T(8,128)(2,1)} %bitcast.14), custom_call_target="tpu_custom_call" | custom-call | tf_op jit(solution)/shard_map/edge_x_kernel/pallas_call | solution.py:627
  4.7 1.5 %collective-permute-start = (bf16[272,256]{1,0:T(8,128)(2,1)}, bf16[272,256]{1,0:T(8,128)(2,1)S(1)}, u32[]{:S(2)}, u32[]{:S(2)}) collective-permute-start(bf16[272,256]{1,0:T(8,128)(2,1)} %get-tuple-element.20), channel_id=1, source_target_pairs={{0,16},{16,0},{32,48},{48,32},{64,80},{80,64},{96,112},{112,96},{1... | collective-permute-start | bytes 417800 | tf_op jit(solution)/shard_map/ppermute | solution.py:592
  6.2 3.1 %collective-permute-start.1 = (bf16[272,256]{1,0:T(8,128)(2,1)}, bf16[272,256]{1,0:T(8,128)(2,1)S(1)}, u32[]{:S(2)}, u32[]{:S(2)}) collective-permute-start(bf16[272,256]{1,0:T(8,128)(2,1)} %get-tuple-element.21), channel_id=1, source_target_pairs={{16,32},{32,16},{48,64},{64,48},{80,96},{96,80},{112,128},{128,112... | collective-permute-start | bytes 417800 | tf_op jit(solution)/shard_map/ppermute | solution.py:592
  9.3 2.5 %edge_v_kernel.1 = (bf16[384,128]{1,0:T(8,128)(2,1)}, bf16[384,128]{1,0:T(8,128)(2,1)}) custom-call(s32[20]{0:T(128)} %concatenate.3.s_ref, f32[3,512,256]{2,1,0:T(8,128)} %bitcast.12), custom_call_target="tpu_custom_call" | custom-call | tf_op jit(solution)/shard_map/edge_v_kernel/pallas_call | solution.py:630
  11.9 8.7 %collective-permute-done.1.xo_ref = bf16[272,256]{1,0:T(8,128)(2,1)S(1)} collective-permute-done((bf16[272,256]{1,0:T(8,128)(2,1)}, bf16[272,256]{1,0:T(8,128)(2,1)S(1)}, u32[]{:S(2)}, u32[]{:S(2)}) %collective-permute-start.1) | collective-permute-done | bytes 139296 | tf_op jit(solution)/shard_map/ppermute | solution.py:592
  21.2 2.2 %edge_y_kernel.1 = (bf16[688,128]{1,0:T(8,128)(2,1)}, bf16[688,128]{1,0:T(8,128)(2,1)}) custom-call(s32[20]{0:T(128)} %concatenate.3.s_ref, bf16[512,256]{1,0:T(8,128)(2,1)} %bitcast.18, bf16[512,256]{1,0:T(8,128)(2,1)} %bitcast.15, bf16[272,256]{1,0:T(8,128)(2,1)} %copy-done, bf16[272,256]{1,0:T(8,128)(2,1)} %copy-done.1, ...), custom_call_target="tpu_custom_call" | custom-call | tf_op jit(solution)/shard_map/edge_y_kernel/pallas_call | solution.py:632
  24.1 1.0 collective-permute-done.2.ye_ref
  25.7 0.7 copy-done.3
  26.4 8.2 %warp_kernel.1 = (bf16[32,16,384]{2,1,0:T(8,128)(2,1)}, f32[3,32,16,384]{3,2,1,0:T(8,128)}, bf16[8,16,384]{2,1,0:T(8,128)(2,1)}, bf16[8,16,384]{2,1,0:T(8,128)(2,1)}) custom-call(s32[20]{0:T(128)} %concatenate.3.s_ref, bf16[512,256]{1,0:T(8,128)(2,1)} %bitcast.19, bf16[272,256]{1,0:T(8,128)(2,1)} %copy-done, bf16[272,256]{1,0:T(8,128)(2,1)} %copy-done.1, ...), custom_call_target="tpu_custom_call" | custom-call | tf_op jit(solution)/shard_map/warp_kernel/pallas_call | solution.py:636
  34.7 3.4 %collective-permute-start.5 = (bf16[8,16,384]{2,1,0:T(8,128)(2,1)}, bf16[8,16,384]{2,1,0:T(8,128)(2,1)S(1)}, u32[]{:S(2)}, u32[]{:S(2)}) collective-permute-start(bf16[8,16,384]{2,1,0:T(8,128)(2,1)} %get-tuple-element.28), channel_id=1, source_target_pairs={{16,32},{32,16},{48,64},{64,48},{80,96},{96,80},{112,128},{128,112... | collective-permute-start | bytes 294920 | tf_op jit(solution)/shard_map/ppermute | solution.py:592
  39.4 9.2 %window_kernel.1 = (bf16[48,16,384]{2,1,0:T(8,128)(2,1)}, f32[2,3,640,128]{3,2,1,0:T(8,128)}, f32[3,40,128]{2,1,0:T(8,128)}, f32[3,3,512,128]{3,2,1,0:T(8,128)}) custom-call(s32[20]{0:T(128)} %concatenate.3.s_ref, bf16[512,256]{1,0:T(8,128)(2,1)} %bitcast.16, bf16[272,256]{1,0:T(8,128)(2,1)} %copy-done, bf16[272,256]{1,0:T(8,128)(2,1)} %copy-done.1, ...), custom_call_target="tpu_custom_call" | custom-call | tf_op jit(solution)/shard_map/window_kernel/pallas_call | solution.py:652
  49.3 12.7 %gradient_kernel.1 = (f32[3,32,16,256]{3,2,1,0:T(8,128)}, bf16[3,7,16,256]{3,2,1,0:T(8,128)(2,1)}, bf16[3,7,16,256]{3,2,1,0:T(8,128)(2,1)}, f32[16,128]{1,0:T(8,128)}) custom-call(s32[20]{0:T(128)} %concatenate.3.s_ref, bf16[32,16,384]{2,1,0:T(8,128)(2,1)} %get-tuple-element.26.w_ref, bf16[8,16,384]{2,1,0:T(8,128)(2,1)} %copy-done.6, ...), custom_call_target="tpu_custom_call" | custom-call | tf_op jit(solution)/shard_map/gradient_kernel/pallas_call | solution.py:666
  62.0 1.3 %reduce_sum.27 = f32[]{:T(128)} reduce(f32[16,128]{1,0:T(8,128)} %get-tuple-element.37, f32[]{:T(128)} %constant.21.clone.1), dimensions={0,1}, to_apply=%region_0.0 | reduce | flops 2047 | bytes 8200 | tf_op jit(solution)/shard_map/reduce_sum | solution.py:681
  63.3 0.7 fusion
  64.0 0.7 broadcast_in_dim.2
  64.7 19.8 %all-to-all-start = ((f32[256,1,128]{2,1,0:T(1,128)}), f32[256,1,128]{2,1,0:T(1,128)S(1)}, u32[]{:S(2)}, u32[]{:S(2)}) async-start(f32[256,1,128]{2,1,0:T(1,128)} %broadcast_in_dim.2), calls=%async_computation | async-start | bytes 262144 | tf_op jit(solution)/shard_map/all_to_all | solution.py:683
  84.5 1.6 %collective-permute-start.6 = (bf16[3,7,16,256]{3,2,1,0:T(8,128)(2,1)}, bf16[3,7,16,256]{3,2,1,0:T(8,128)(2,1)S(1)}, u32[]{:S(2)}, u32[]{:S(2)}) collective-permute-start(bf16[3,7,16,256]{3,2,1,0:T(8,128)(2,1)} %get-tuple-element.35), channel_id=1, source_target_pairs={{0,16},{16,0},{32,48},{48,32},{64,80},{80,64},{96,112},{112,96},{1... | collective-permute-start | bytes 516104 | tf_op jit(solution)/shard_map/ppermute | solution.py:592
  86.1 3.4 %collective-permute-start.7 = (bf16[3,7,16,256]{3,2,1,0:T(8,128)(2,1)}, bf16[3,7,16,256]{3,2,1,0:T(8,128)(2,1)S(1)}, u32[]{:S(2)}, u32[]{:S(2)}) collective-permute-start(bf16[3,7,16,256]{3,2,1,0:T(8,128)(2,1)} %get-tuple-element.36), channel_id=1, source_target_pairs={{16,32},{32,16},{48,64},{64,48},{80,96},{96,80},{112,128},{128,112... | collective-permute-start | bytes 516104 | tf_op jit(solution)/shard_map/ppermute | solution.py:592
  89.5 1.9 %collective-permute-done.6.ge_ref = bf16[3,7,16,256]{3,2,1,0:T(8,128)(2,1)S(1)} collective-permute-done((bf16[3,7,16,256]{3,2,1,0:T(8,128)(2,1)}, bf16[3,7,16,256]{3,2,1,0:T(8,128)(2,1)S(1)}, u32[]{:S(2)}, u32[]{:S(2)}) %collective-permute-start.6) | collective-permute-done | bytes 172064 | tf_op jit(solution)/shard_map/ppermute | solution.py:592
  91.5 10.7 %collective-permute-done.7.go_ref = bf16[3,7,16,256]{3,2,1,0:T(8,128)(2,1)S(1)} collective-permute-done((bf16[3,7,16,256]{3,2,1,0:T(8,128)(2,1)}, bf16[3,7,16,256]{3,2,1,0:T(8,128)(2,1)S(1)}, u32[]{:S(2)}, u32[]{:S(2)}) %collective-permute-start.7) | collective-permute-done | bytes 172064 | tf_op jit(solution)/shard_map/ppermute | solution.py:592
  102.1 0.7 copy-done.5
  102.8 5.3 %smooth_kernel.1 = f32[3,512,256]{2,1,0:T(8,128)} custom-call(s32[20]{0:T(128)} %concatenate.3.s_ref, f32[3,32,16,256]{3,2,1,0:T(8,128)} %get-tuple-element.34.ys_ref, bf16[3,7,16,256]{3,2,1,0:T(8,128)(2,1)} %copy-done.4, bf16[3,7,16,256]{3,2,1,0:T(8,128)(2,1)} %copy-done.5), custom_call_target="tpu_custom_call" | custom-call | tf_op jit(solution)/shard_map/smooth_kernel/pallas_call | solution.py:687
  (29 shorter events, 4.8 us)
Async XLA Ops:
  4.7 7.1 %collective-permute-start = (bf16[272,256]{1,0:T(8,128)(2,1)}, bf16[272,256]{1,0:T(8,128)(2,1)S(1)}, u32[]{:S(2)}, u32[]{:S(2)}) collective-permute-start(bf16[272,256]{1,0:T(8,128)(2,1)} %get-tuple-element.20), channel_id=1, source_target_pairs={{0,16},{16,0},{32,48},{48,32},{64,80},{80,64},{96,112},{112,96},{1... | collective-permute-start | bytes 417800 | tf_op jit(solution)/shard_map/ppermute | solution.py:592
  6.2 14.3 %collective-permute-start.1 = (bf16[272,256]{1,0:T(8,128)(2,1)}, bf16[272,256]{1,0:T(8,128)(2,1)S(1)}, u32[]{:S(2)}, u32[]{:S(2)}) collective-permute-start(bf16[272,256]{1,0:T(8,128)(2,1)} %get-tuple-element.21), channel_id=1, source_target_pairs={{16,32},{32,16},{48,64},{64,48},{80,96},{96,80},{112,128},{128,112... | collective-permute-start | bytes 417800 | tf_op jit(solution)/shard_map/ppermute | solution.py:592
  11.9 26.2 %copy-start.8 = (s32[2,2]{1,0:T(2,128)S(1)}, s32[2,2]{1,0:T(2,128)}, u32[]{:S(2)}) copy-start(s32[2,2]{1,0:T(2,128)} %param.11) | copy-start | bytes 52
  11.9 8.7 %copy-start = (bf16[272,256]{1,0:T(8,128)(2,1)}, bf16[272,256]{1,0:T(8,128)(2,1)S(1)}, u32[]{:S(2)}) copy-start(bf16[272,256]{1,0:T(8,128)(2,1)S(1)} %collective-permute-done.xe_ref) | copy-start | bytes 417796
  20.5 0.7 copy-start.1
  23.4 1.6 %collective-permute-start.2 = (bf16[688,128]{1,0:T(8,128)(2,1)}, bf16[688,128]{1,0:T(8,128)(2,1)S(1)}, u32[]{:S(2)}, u32[]{:S(2)}) collective-permute-start(bf16[688,128]{1,0:T(8,128)(2,1)} %get-tuple-element.24), channel_id=1, source_target_pairs={{0,1},{1,0},{2,3},{3,2},{4,5},{5,4},{6,7},{7,6},{8,9},{9,8},{10,11... | collective-permute-start | bytes 528392 | tf_op jit(solution)/shard_map/ppermute | solution.py:592
  23.4 1.6 %collective-permute-start.3 = (bf16[688,128]{1,0:T(8,128)(2,1)}, bf16[688,128]{1,0:T(8,128)(2,1)S(1)}, u32[]{:S(2)}, u32[]{:S(2)}) collective-permute-start(bf16[688,128]{1,0:T(8,128)(2,1)} %get-tuple-element.25), channel_id=1, source_target_pairs={{1,2},{2,1},{3,4},{4,3},{5,6},{6,5},{7,8},{8,7},{9,10},{10,9},{11,... | collective-permute-start | bytes 528392 | tf_op jit(solution)/shard_map/ppermute | solution.py:592
  25.0 0.7 copy-start.2
  25.7 0.7 copy-start.3
  34.6 14.0 %collective-permute-start.4 = (bf16[8,16,384]{2,1,0:T(8,128)(2,1)}, bf16[8,16,384]{2,1,0:T(8,128)(2,1)S(1)}, u32[]{:S(2)}, u32[]{:S(2)}) collective-permute-start(bf16[8,16,384]{2,1,0:T(8,128)(2,1)} %get-tuple-element.27), channel_id=1, source_target_pairs={{0,16},{16,0},{32,48},{48,32},{64,80},{80,64},{96,112},{112,96},{1... | collective-permute-start | bytes 294920 | tf_op jit(solution)/shard_map/ppermute | solution.py:592
  34.7 13.9 %collective-permute-start.5 = (bf16[8,16,384]{2,1,0:T(8,128)(2,1)}, bf16[8,16,384]{2,1,0:T(8,128)(2,1)S(1)}, u32[]{:S(2)}, u32[]{:S(2)}) collective-permute-start(bf16[8,16,384]{2,1,0:T(8,128)(2,1)} %get-tuple-element.28), channel_id=1, source_target_pairs={{16,32},{32,16},{48,64},{64,48},{80,96},{96,80},{112,128},{128,112... | collective-permute-start | bytes 294920 | tf_op jit(solution)/shard_map/ppermute | solution.py:592
  48.6 0.6 copy-start.6
  48.6 0.7 copy-start.7
  64.7 43.4 %all-to-all-start = ((f32[256,1,128]{2,1,0:T(1,128)}), f32[256,1,128]{2,1,0:T(1,128)S(1)}, u32[]{:S(2)}, u32[]{:S(2)}) async-start(f32[256,1,128]{2,1,0:T(1,128)} %broadcast_in_dim.2), calls=%async_computation | async-start | bytes 262144 | tf_op jit(solution)/shard_map/all_to_all | solution.py:683
  84.5 7.0 %collective-permute-start.6 = (bf16[3,7,16,256]{3,2,1,0:T(8,128)(2,1)}, bf16[3,7,16,256]{3,2,1,0:T(8,128)(2,1)S(1)}, u32[]{:S(2)}, u32[]{:S(2)}) collective-permute-start(bf16[3,7,16,256]{3,2,1,0:T(8,128)(2,1)} %get-tuple-element.35), channel_id=1, source_target_pairs={{0,16},{16,0},{32,48},{48,32},{64,80},{80,64},{96,112},{112,96},{1... | collective-permute-start | bytes 516104 | tf_op jit(solution)/shard_map/ppermute | solution.py:592
  86.1 16.1 %collective-permute-start.7 = (bf16[3,7,16,256]{3,2,1,0:T(8,128)(2,1)}, bf16[3,7,16,256]{3,2,1,0:T(8,128)(2,1)S(1)}, u32[]{:S(2)}, u32[]{:S(2)}) collective-permute-start(bf16[3,7,16,256]{3,2,1,0:T(8,128)(2,1)} %get-tuple-element.36), channel_id=1, source_target_pairs={{16,32},{32,16},{48,64},{64,48},{80,96},{96,80},{112,128},{128,112... | collective-permute-start | bytes 516104 | tf_op jit(solution)/shard_map/ppermute | solution.py:592
  91.5 10.7 %copy-start.4 = (bf16[3,7,16,256]{3,2,1,0:T(8,128)(2,1)}, bf16[3,7,16,256]{3,2,1,0:T(8,128)(2,1)S(1)}, u32[]{:S(2)}) copy-start(bf16[3,7,16,256]{3,2,1,0:T(8,128)(2,1)S(1)} %collective-permute-done.6.ge_ref) | copy-start | bytes 516100
  102.1 0.7 copy-start.5

commit v2 on v1

--- a/solution.py
+++ b/solution.py
@@ -1,4 +1,3 @@
-import functools
 import math
 
 import jax
@@ -8,6 +7,7 @@
 from jax.experimental import pallas as pl
 from jax.experimental.pallas import tpu as pltpu
 from jax.sharding import PartitionSpec as P
+
 
 DEPTH = 16
 BX = 16
@@ -25,11 +25,10 @@
 F32 = jnp.float32
 BF16 = jnp.bfloat16
 
+VMEM_LIMIT = 28 << 20
 VMEM_SPEC = pl.BlockSpec(memory_space=pltpu.VMEM)
 SMEM_SPEC = pl.BlockSpec(memory_space=pltpu.SMEM)
-ANY_SPEC = pl.BlockSpec(memory_space=pl.ANY)
-
-PX, PY, HAS_L, HAS_R, OFF, TIS = 0, 1, 2, 3, 4, 16
+ANY_SPEC = pl.BlockSpec(memory_space=pltpu.HBM)
 
 
 def gauss_weights():
@@ -84,24 +83,32 @@
     return x.reshape(DEPTH, rows, x.shape[-1])
 
 
-def edge_x_kernel(s_ref, m_ref, f_ref, e_ref, o_ref):
-    px = s_ref[PX]
+def edge_x_kernel(t_hbm, m_hbm, f_hbm, e_ref, o_ref, t_scr, m_scr, f_scr, sem):
+    copies = [
+        pltpu.make_async_copy(src, dst, sem.at[i])
+        for i, (src, dst) in enumerate(((m_hbm, m_scr), (f_hbm, f_scr), (t_hbm, t_scr)))
+    ]
+    for copy in copies:
+        copy.start()
+    px = lax.axis_index("gx") & 1
     lane = lane_iota((16, 2 * LANES))
-    for n, ref in enumerate((m_ref, f_ref)):
+    for n, ref in enumerate((m_scr, f_scr)):
+        copies[n].wait()
         v = planes(ref[...].astype(F32), ROWS)
         first = v[:, :8].reshape(128, 2 * LANES)
         last = v[:, 24:].reshape(128, 2 * LANES)
         e_ref[128 * n : 128 * n + 128] = pick(px, last, first).astype(BF16)
         o_ref[128 * n : 128 * n + 128] = pick(px, first, last).astype(BF16)
-    t = [[s_ref[TIS + 2 * i + j].astype(F32) for j in range(2)] for i in range(2)]
+    copies[2].wait()
+    t = [[t_scr[i, j].astype(F32) for j in range(2)] for i in range(2)]
     first = jnp.where(lane < LANES, t[0][0], t[0][1])
     last = jnp.where(lane < LANES, t[1][0], t[1][1])
     e_ref[256:272] = pick(px, last, first).astype(BF16)
     o_ref[256:272] = pick(px, first, last).astype(BF16)
 
 
-def edge_v_kernel(s_ref, v_ref, e_ref, o_ref):
-    py = s_ref[PY]
+def edge_v_kernel(v_ref, e_ref, o_ref):
+    py = lax.axis_index("gy") & 1
     for c in range(3):
         first = pack_edge(v_ref[c, :, :LANES], 8, False)
         last = pack_edge(v_ref[c, :, LANES:], 8, True)
@@ -124,9 +131,9 @@
     )
 
 
-def edge_y_kernel(s_ref, m_ref, f_ref, xe_ref, xo_ref, ve_ref, vo_ref, e_ref, o_ref):
-    px = s_ref[PX]
-    py = s_ref[PY]
+def edge_y_kernel(off_ref, t_ref, m_ref, f_ref, xe_ref, xo_ref, ve_ref, vo_ref, e_ref, o_ref):
+    px = lax.axis_index("gx") & 1
+    py = lax.axis_index("gy") & 1
     row = 0
     for n, (ref, groups) in enumerate(((m_ref, 4), (f_ref, 8))):
         ext = extended(ref[...], xe_ref, xo_ref, px, 128 * n).reshape(DEPTH * EXT, 2 * LANES)
@@ -146,11 +153,11 @@
         acc = jnp.zeros((16, LANES), F32)
         for c in range(3):
             for i in range(2):
-                acc = jnp.where(lane == 2 * c + i, s_ref[OFF + 4 * c + 2 * i + j].astype(F32), acc)
+                acc = jnp.where(lane == 2 * c + i, off_ref[c, i, j].astype(F32), acc)
         tissue = (
             before[:, LANES * j : LANES * j + LANES],
-            s_ref[TIS + j].astype(F32),
-            s_ref[TIS + 2 + j].astype(F32),
+            t_ref[0, j].astype(F32),
+            t_ref[1, j].astype(F32),
             after[:, LANES * j : LANES * j + LANES],
         )
         for i, t in enumerate(tissue):
@@ -171,12 +178,12 @@
 
 
 def warp_kernel(
-    s_ref, m_ref, xe_ref, xo_ref, ye_ref, yo_ref, v_hbm,
+    off_ref, m_ref, xe_ref, xo_ref, ye_ref, yo_ref, v_hbm,
     w_ref, slope_ref, e_ref, o_ref,
     m_scr, v_scr, r_scr, sem,
 ):
-    px = s_ref[PX]
-    py = s_ref[PY]
+    px = lax.axis_index("gx") & 1
+    py = lax.axis_index("gy") & 1
     copies = []
     for c in range(3):
         for j in range(2):
@@ -271,7 +278,7 @@
         copy.wait()
     for j in range(2):
         for xb in range(2):
-            gather(j, xb, *(s_ref[OFF + 4 * c + 2 * xb + j] for c in range(3)), False)
+            gather(j, xb, *(off_ref[c, xb, j] for c in range(3)), False)
             blend(j, xb)
     e_ref[...] = w_ref[pl.ds(jnp.where(px == 0, ROWS - 8, 0), 8)]
     o_ref[...] = w_ref[pl.ds(jnp.where(px == 0, 0, ROWS - 8), 8)]
@@ -297,7 +304,7 @@
     return total
 
 
-def box_z(v):
+def box_column(v):
     three = {z: add_all([v[i] for i in (z - 1, z, z + 1) if 0 <= i < DEPTH]) for z in range(-3, 19)}
     return [add_all([three[z - 3], three[z], three[z + 3]]) for z in range(DEPTH)]
 
@@ -324,23 +331,23 @@
         ref[q, j, pl.ds(first, v.shape[0]), :] = v[:, LANES * j : LANES * j + LANES]
 
 
-def box_z_in_place(ref, q, count):
+def box_z(src, dst, q, count):
     @pl.loop(0, count // 8)
     def _(t):
         for j in range(3):
             rows = [pl.ds(t * 128 + z, 8, stride=DEPTH) for z in range(DEPTH)]
-            v = box_z([ref[q, j, r, :] for r in rows])
+            v = box_column([src[q, j, r, :] for r in rows])
             for z in range(DEPTH):
-                ref[q, j, rows[z], :] = v[z]
+                dst[q, j, rows[z], :] = v[z]
 
 
 def window_kernel(
-    s_ref, f_ref, xe_ref, xo_ref, ye_ref, yo_ref, w_ref, band_ref,
+    t_ref, f_ref, xe_ref, xo_ref, ye_ref, yo_ref, w_ref, band_ref,
     fx_ref, sum_ref, mask_ref, own_ref,
     f_scr, y_scr,
 ):
-    px = s_ref[PX]
-    py = s_ref[PY]
+    px = lax.axis_index("gx") & 1
+    py = lax.axis_index("gy") & 1
     ext = extended(f_ref[...], xe_ref, xo_ref, px, 128).reshape(DEPTH * EXT, 2 * LANES)
     f_scr[0] = ext[:, :LANES]
     f_scr[1] = ext[:, LANES:]
@@ -362,8 +369,8 @@
             lanes = slice(LANES * j, LANES * j + LANES)
             t = [
                 before[:1, lanes],
-                jnp.full((1, LANES), s_ref[TIS + j].astype(F32)),
-                jnp.full((1, LANES), s_ref[TIS + 2 + j].astype(F32)),
+                jnp.full((1, LANES), t_ref[0, j].astype(F32)),
+                jnp.full((1, LANES), t_ref[1, j].astype(F32)),
                 after[:1, lanes],
             ]
         else:
@@ -389,7 +396,7 @@
         f = fx_ref[x + 8 : x + 24].reshape(256, 3 * LANES)
         image_sums(own_ref, 256 * part, w, f, band)
     for q in range(2):
-        box_z_in_place(y_scr, q, EXT)
+        box_z(y_scr, y_scr, q, EXT)
         for j in range(3):
             def load(x):
                 return y_scr[q, j, DEPTH * x : DEPTH * x + DEPTH]
@@ -399,7 +406,7 @@
 
             box_x(load, store, OUT)
     for q in range(3):
-        box_z_in_place(own_ref, q, ROWS)
+        box_z(own_ref, own_ref, q, ROWS)
 
 
 def image_sums(ref, first, w, f, band):
@@ -409,20 +416,19 @@
     put_tiles(ref, 2, first, box_y(split(i * f.astype(F32)), band))
 
 
-def gradient_kernel(
-    s_ref, w_ref, we_ref, wo_ref, fx_ref, sum_ref, mask_ref, own_ref, slope_ref,
-    band_ref, gh_ref, gl_ref,
-    ys_ref, e_ref, o_ref, loss_ref,
-    h_scr, s_scr, a_scr, b_scr,
+def stats_kernel(
+    t_ref, we_ref, wo_ref, fx_ref, sum_ref, mask_ref, own_ref, band_ref,
+    a_ref, share_ref,
+    h_scr, s_scr, n_scr,
 ):
-    px = s_ref[PX]
+    px = lax.axis_index("gx") & 1
     band = band_ref[...]
     before, after = before_after(px, we_ref[...].astype(F32), wo_ref[...].astype(F32))
     w = jnp.concatenate([before, after], axis=0).astype(BF16).reshape(256, 3 * LANES)
     f = jnp.concatenate([fx_ref[0:8], fx_ref[40:48]], axis=0).reshape(256, 3 * LANES)
     image_sums(h_scr, 0, w, f, band)
     for q in range(3):
-        box_z_in_place(h_scr, q, 16)
+        box_z(h_scr, h_scr, q, 16)
 
     @pl.loop(0, 3)
     def _(j):
@@ -461,14 +467,14 @@
                 -2.0 * m * quotient,
             )
             for k in range(3):
-                a_scr[k, j, rows, :] = adjoint[k] if j < 2 else jnp.where(near, adjoint[k], 0.0)
+                a_ref[k, j, rows, :] = adjoint[k] if j < 2 else jnp.where(near, adjoint[k], 0.0)
             if inner and j < 2:
                 ncc = m * (cross * quotient)
                 total = ncc if total is None else total + ncc
         if inner:
-            loss_ref[...] += total
-
-    loss_ref[...] = jnp.zeros((DEPTH, LANES), F32)
+            n_scr[...] += total
+
+    n_scr[...] = jnp.zeros((DEPTH, LANES), F32)
 
     @pl.loop(0, ROWS, unroll=2)
     def _(x):
@@ -477,8 +483,20 @@
     for x in (0, 1, 2, 3, 36, 37, 38, 39):
         stats(x, False)
 
+    blocks = (t_ref[0, 0] + t_ref[0, 1] + t_ref[1, 0] + t_ref[1, 1]).astype(F32)
+    column = lane_iota(share_ref.shape)
+    share_ref[...] = jnp.where(column == 0, jnp.sum(n_scr[...]), jnp.where(column == 1, blocks, 0.0))
+
+
+def gradient_kernel(
+    a_ref, w_ref, fx_ref, slope_ref, band_ref, gh_ref, gl_ref,
+    ys_ref, e_ref, o_ref,
+    a_scr, b_scr,
+):
+    px = lax.axis_index("gx") & 1
+    band = band_ref[...]
     for k in range(3):
-        box_z_in_place(a_scr, k, OUT)
+        box_z(a_ref, a_scr, k, OUT)
 
     for j in range(3):
         lanes = slice(LANES * j, LANES * j + LANES)
@@ -494,8 +512,8 @@
             box_x(load, store, ROWS)
 
     column = lane_iota((1, 3 * LANES))
-    r_lim = jnp.where(s_ref[HAS_R] == 1, 2 * LANES + GAUSS_RADIUS, 2 * LANES)
-    l_lim = jnp.where(s_ref[HAS_L] == 1, 3 * LANES - GAUSS_RADIUS, 3 * LANES)
+    r_lim = jnp.where(lax.axis_index("gy") < lax.axis_size("gy") - 1, 2 * LANES + GAUSS_RADIUS, 2 * LANES)
+    l_lim = jnp.where(lax.axis_index("gy") > 0, 3 * LANES - GAUSS_RADIUS, 3 * LANES)
     valid = (column < r_lim) | (column >= l_lim)
     gh = gh_ref[...]
     gl = gl_ref[...]
@@ -523,9 +541,9 @@
         o_ref[c] = pick(px, first, last).astype(BF16)
 
 
-def smooth_kernel(s_ref, ys_ref, ge_ref, go_ref, out_hbm, h_scr, z_scr, o_scr, sem):
+def smooth_kernel(ys_ref, ge_ref, go_ref, all_ref, out_hbm, loss_ref, h_scr, z_scr, o_scr, sem):
     weights = gauss_weights()
-    px = s_ref[PX]
+    px = lax.axis_index("gx") & 1
     r = GAUSS_RADIUS
     for c in range(3):
         before, after = before_after(px, ge_ref[c].astype(F32), go_ref[c].astype(F32))
@@ -568,18 +586,24 @@
             )
             copy.start()
             copies.append(copy)
+    column = lane_iota(all_ref.shape)
+    shares = all_ref[...]
+    total = jnp.sum(jnp.where(column == 0, shares, 0.0))
+    blocks = jnp.sum(jnp.where(column == 1, shares, 0.0))
+    row = jnp.full((1, LANES), -total) / (jnp.full((1, LANES), blocks) * float(BX * BY * DEPTH))
+    loss_ref[...] = row
     for copy in copies:
         copy.wait()
 
 
-def call(kernel, outs, in_specs, out_specs, scratch=()):
+def call(kernel, outs, in_specs, out_specs, scratch=(), limit=VMEM_LIMIT):
     return pl.pallas_call(
         kernel,
         out_shape=tuple(jax.ShapeDtypeStruct(s, d) for s, d in outs),
         in_specs=list(in_specs),
         out_specs=tuple(out_specs),
         scratch_shapes=list(scratch),
-        name=kernel.__name__,
+        compiler_params=pltpu.CompilerParams(vmem_limit_bytes=limit),
     )
 
 
@@ -589,7 +613,9 @@
     second = []
     for i in range(1, count - 1, 2):
         second += [(i, i + 1), (i + 1, i)]
-    return lax.ppermute(even, axis, first), lax.ppermute(odd, axis, second)
+    even = lax.ppermute(even, axis, first)
+    odd = lax.ppermute(odd, axis, second)
+    return even, odd
 
 
 def matrices():
@@ -607,16 +633,7 @@
     return hi, lo, jnp.asarray(band).astype(BF16)
 
 
-def on_device(moving_image, fixed_image, velocity, offsets, tissue):
-    ix, iy = lax.axis_index("gx"), lax.axis_index("gy")
-    ny = lax.axis_size("gy")
-    table = jnp.concatenate(
-        [
-            jnp.stack([ix & 1, iy & 1, (iy > 0).astype(jnp.int32), (iy < ny - 1).astype(jnp.int32)]),
-            offsets.reshape(12),
-            tissue.reshape(4),
-        ]
-    ).astype(jnp.int32)
+def step(moving_image, fixed_image, velocity, offsets, tissue):
     rows = DEPTH * ROWS
     m = moving_image.reshape(rows, 2 * LANES)
     f = fixed_image.reshape(rows, 2 * LANES)
@@ -624,12 +641,26 @@
 
     V, S, A = VMEM_SPEC, SMEM_SPEC, ANY_SPEC
     edge = ((272, 2 * LANES), BF16)
-    xe, xo = call(edge_x_kernel, [edge, edge], [S, V, V], [V, V])(table, m, f)
+    xe, xo = call(
+        edge_x_kernel,
+        [edge, edge],
+        [A] * 3,
+        [V] * 2,
+        [
+            pltpu.SMEM((2, 2), jnp.int32),
+            pltpu.VMEM((rows, 2 * LANES), BF16),
+            pltpu.VMEM((rows, 2 * LANES), BF16),
+            pltpu.SemaphoreType.DMA((3,)),
+        ],
+        60 << 20,
+    )(tissue, m, f)
     rxe, rxo = swap("gx", xe, xo)
     edge = ((384, LANES), BF16)
-    ve, vo = call(edge_v_kernel, [edge, edge], [S, V], [V, V])(table, v)
+    ve, vo = call(edge_v_kernel, [edge, edge], [V], [V, V])(v)
     edge = ((Y_ROWS, LANES), BF16)
-    ye, yo = call(edge_y_kernel, [edge, edge], [S] + [V] * 6, [V, V])(table, m, f, rxe, rxo, ve, vo)
+    ye, yo = call(edge_y_kernel, [edge, edge], [S, S] + [V] * 6, [V, V])(
+        offsets, tissue, m, f, rxe, rxo, ve, vo
+    )
     rye, ryo = swap("gy", ye, yo)
 
     edge = ((8, DEPTH, 3 * LANES), BF16)
@@ -644,7 +675,7 @@
             pltpu.VMEM((2, 2, BX + 1, DEPTH, LANES), F32),
             pltpu.SemaphoreType.DMA((6,)),
         ],
-    )(table, m, rxe, rxo, rye, ryo, v)
+    )(offsets, m, rxe, rxo, rye, ryo, v)
     rwe, rwo = swap("gx", we, wo)
 
     gh, gl, band = matrices()
@@ -660,43 +691,54 @@
         [S] + [V] * 7,
         [V] * 4,
         [pltpu.VMEM((3, DEPTH * EXT, LANES), F32), pltpu.VMEM((2, 3, DEPTH * EXT, LANES), F32)],
-    )(table, f, rxe, rxo, rye, ryo, w, band)
-
-    edge = ((3, GAUSS_RADIUS, DEPTH, 2 * LANES), BF16)
-    ys, ge, go, loss = call(
-        gradient_kernel,
-        [((3, ROWS, DEPTH, 2 * LANES), F32), edge, edge, ((DEPTH, LANES), F32)],
-        [S] + [V] * 11,
-        [V] * 4,
+    )(tissue, f, rxe, rxo, rye, ryo, w, band)
+
+    adjoint = ((3, 3, DEPTH * OUT, LANES), F32)
+    adj, share = call(
+        stats_kernel,
+        [adjoint, ((8, LANES), F32)],
+        [S] + [V] * 7,
+        [V] * 2,
         [
             pltpu.VMEM((3, 3, 256, LANES), F32),
-            pltpu.VMEM((3, 3, DEPTH * OUT, LANES), F32),
-            pltpu.VMEM((3, 3, DEPTH * OUT, LANES), F32),
-            pltpu.VMEM((3, 2, ROWS, DEPTH, 3 * LANES), BF16),
+            pltpu.VMEM(*adjoint),
+            pltpu.VMEM((DEPTH, LANES), F32),
         ],
-    )(table, w, rwe, rwo, fx, sums, mask, own, slope, band, gh, gl)
+    )(tissue, rwe, rwo, fx, sums, mask, own, band)
+
+    edge = ((3, GAUSS_RADIUS, DEPTH, 2 * LANES), BF16)
+    ys, ge, go = call(
+        gradient_kernel,
+        [((3, ROWS, DEPTH, 2 * LANES), F32), edge, edge],
+        [V] * 7,
+        [V] * 3,
+        [pltpu.VMEM(*adjoint), pltpu.VMEM((3, 2, ROWS, DEPTH, 3 * LANES), BF16)],
+    )(adj, w, fx, slope, band, gh, gl)
     rge, rgo = swap("gx", ge, go)
 
-    devices = lax.axis_size("gx") * ny
-    local = jnp.stack([jnp.sum(loss), jnp.sum(tissue).astype(F32)])
-    line = jnp.pad(local, (0, LANES - 2)).reshape(1, 1, LANES)
-    everyone = lax.all_to_all(jnp.broadcast_to(line, (devices, 1, LANES)), ("gx", "gy"), 0, 0)
-    totals = jnp.sum(everyone, axis=(0, 1))
-    similarity_loss = -totals[0] / (totals[1] * float(BX * BY * DEPTH))
-
-    (update,) = call(
+    nx, ny = lax.axis_size("gx"), lax.axis_size("gy")
+    other = lax.ppermute(share, "gy", [(i, i ^ 1) for i in range(ny)])
+    line = (share[:1] + other[:1]).reshape(1, 1, LANES)
+    groups = [[i * ny + j for i in range(nx) for j in range(p, ny, 2)] for p in range(2)]
+    count = nx * ny // 2
+    everyone = lax.all_to_all(
+        jnp.broadcast_to(line, (count, 1, LANES)), ("gx", "gy"), 0, 0, axis_index_groups=groups
+    )
+    everyone = everyone.reshape(count, LANES)
+
+    update, loss = call(
         smooth_kernel,
-        [((3, rows, 2 * LANES), F32)],
-        [S] + [V] * 3,
-        [A],
+        [((3, rows, 2 * LANES), F32), ((1, LANES), F32)],
+        [V] * 4,
+        [A, V],
         [
             pltpu.VMEM((2, 3, GAUSS_RADIUS, DEPTH, 2 * LANES), F32),
             pltpu.VMEM((rows, LANES), F32),
             pltpu.VMEM((3, 2, rows, LANES), F32),
             pltpu.SemaphoreType.DMA((6,)),
         ],
-    )(table, ys, rge, rgo)
-    return update.reshape(velocity.shape), similarity_loss
+    )(ys, rge, rgo, everyone)
+    return update.reshape(velocity.shape), loss[0, 0]
 
 
 def solution(mesh):
@@ -708,6 +750,4 @@
         P("gx", "gy"),
     )
     out_specs = (P(None, None, "gx", "gy"), P())
-    return jax.shard_map(
-        on_device, mesh=mesh, in_specs=in_specs, out_specs=out_specs, check_vma=False
-    )
+    return jax.shard_map(step, mesh=mesh, in_specs=in_specs, out_specs=out_specs, check_vma=False)

time: 112 us -> 88.6 us (0.79)
  the two profiles are of different devices: /device:TPU:128 before, /device:TPU:1 now
where the time goes in v2:
time: 88.6 us; the launch traced here: 88.3 us
  blocking collectives  30.5 us (34%)
  Pallas kernels  28.4 us (32%)
  starting transfers between devices  21.3 us (24%)
  waiting for transfers between devices  4.85 us (5%)
  local copies, waits for them, and re-layouts  2.26 us (3%)
  between operations  1.04 us (1%)
    all_to_all x1, blocking collectives, step(): lax.all_to_all(jnp.broadcast_to(line, (count, 1, LANES)), ('gx', 'gy'), 0...  30.5 us
    ppermute x4, starting transfers between devices, swap(): even = lax.ppermute(even, axis, first)  17.1 us
    pallas_call x1, Pallas kernels, step(): call(warp_kernel, [((ROWS, DEPTH, 3 * LANES), BF16), ((3, ROWS, DEPTH, 3...  6.15 us
    pallas_call x1, Pallas kernels, step(): call(window_kernel, [((EXT, DEPTH, 3 * LANES), BF16), ((2, 3, DEPTH * OUT...  6.11 us
    pallas_call x1, Pallas kernels, step(): call(gradient_kernel, [((3, ROWS, DEPTH, 2 * LANES), F32), edge, edge], [...  5.27 us
    ppermute x4, waiting for transfers between devices, swap(): odd = lax.ppermute(odd, axis, second)  4.84 us
    pallas_call x1, Pallas kernels, step(): call(smooth_kernel, [((3, rows, 2 * LANES), F32), ((1, LANES), F32)], [V]...  4.31 us
    ppermute x4, starting transfers between devices, swap(): odd = lax.ppermute(odd, axis, second)  3.88 us
  transfers between devices with their start and end apart: 9, of which 1 were waited for; matrix products, arithmetic and copies ran while one was open for 1% of the time, Pallas kernels for 13%

profile of v2, /device:TPU:1, one launch (start us, length us, event | category | flops | bytes accessed | tf_op | source)
XLA Modules:
  0.0 88.3 jit_solution(1250580372025972001)
XLA Ops:
  0.7 1.8 %shard_map.86 = (bf16[272,256]{1,0:T(8,128)(2,1)}, bf16[272,256]{1,0:T(8,128)(2,1)}) custom-call(s32[2,2]{1,0:T(2,128)} %t_ref.5, bf16[512,256]{1,0:T(8,128)(2,1)} %bitcast.14, bf16[512,256]{1,0:T(8,128)(2,1)} %bitcast.11), custom_call_target="tpu_custom_call" | custom-call | tf_op jit(solution)/shard_map/pallas_call | solution.py:644
  2.5 2.1 %collective-permute-start = (bf16[272,256]{1,0:T(8,128)(2,1)}, bf16[272,256]{1,0:T(8,128)(2,1)S(1)}, u32[]{:S(2)}, u32[]{:S(2)}) collective-permute-start(bf16[272,256]{1,0:T(8,128)(2,1)} %get-tuple-element.23), channel_id=1, source_target_pairs={{0,16},{16,0},{32,48},{48,32},{64,80},{80,64},{96,112},{112,96},{1... | collective-permute-start | bytes 417800 | tf_op jit(solution)/shard_map/ppermute | solution.py:616
  4.6 0.7 collective-permute-start.1
  5.3 0.8 copy.12.off_ref
  6.1 1.4 %copy-done = f32[3,16,32,256]{3,2,1,0:T(8,128)S(1)} copy-done((f32[3,16,32,256]{3,2,1,0:T(8,128)S(1)}, f32[3,16,32,256]{3,2,1,0:T(8,128)}, u32[]{:S(2)}) %copy-start) | copy-done | bytes 1572888
  7.5 0.4 shard_map.87
  7.9 0.0 copy-start.2
  8.0 0.9 shard_map.88
  8.8 3.2 %collective-permute-start.2 = (bf16[688,128]{1,0:T(8,128)(2,1)S(1)}, bf16[688,128]{1,0:T(8,128)(2,1)S(1)}, u32[]{:S(2)}, u32[]{:S(2)}) collective-permute-start(bf16[688,128]{1,0:T(8,128)(2,1)S(1)} %get-tuple-element.27), channel_id=1, source_target_pairs={{0,1},{1,0},{2,3},{3,2},{4,5},{5,4},{6,7},{7,6},{8,9},{9,8},{10,11... | collective-permute-start | bytes 528392 | tf_op jit(solution)/shard_map/ppermute | solution.py:616
  12.0 1.9 %collective-permute-start.3 = (bf16[688,128]{1,0:T(8,128)(2,1)S(1)}, bf16[688,128]{1,0:T(8,128)(2,1)S(1)}, u32[]{:S(2)}, u32[]{:S(2)}) collective-permute-start(bf16[688,128]{1,0:T(8,128)(2,1)S(1)} %get-tuple-element.28), channel_id=1, source_target_pairs={{1,2},{2,1},{3,4},{4,3},{5,6},{6,5},{7,8},{8,7},{9,10},{10,9},{11,... | collective-permute-start | bytes 528392 | tf_op jit(solution)/shard_map/ppermute | solution.py:617
  14.0 4.8 %collective-permute-done.3.yo_ref = bf16[688,128]{1,0:T(8,128)(2,1)S(1)} collective-permute-done((bf16[688,128]{1,0:T(8,128)(2,1)S(1)}, bf16[688,128]{1,0:T(8,128)(2,1)S(1)}, u32[]{:S(2)}, u32[]{:S(2)}) %collective-permute-start.3) | collective-permute-done | bytes 176160 | tf_op jit(solution)/shard_map/ppermute | solution.py:617
  18.8 6.2 %shard_map.89 = (bf16[32,16,384]{2,1,0:T(8,128)(2,1)S(1)}, f32[3,32,16,384]{3,2,1,0:T(8,128)S(1)}, bf16[8,16,384]{2,1,0:T(8,128)(2,1)S(1)}, bf16[8,16,384]{2,1,0:T(8,128)(2,1)S(1)}) custom-call(s32[3,2,2]{2,1,0:T(2,128)S(1)} %copy.12.off_ref, bf16[512,256]{1,0:T(8,128)(2,1)S(1)} %bitcast.16, bf16[272,256]{1,0:T(8,128)(2,1)S(1)} %collective-permute-done.xe_ref, ...), custom_call_target="tpu_custom_call" | custom-call | tf_op jit(solution)/shard_map/pallas_call | solution.py:667
  24.9 3.7 %collective-permute-start.4 = (bf16[8,16,384]{2,1,0:T(8,128)(2,1)S(1)}, bf16[8,16,384]{2,1,0:T(8,128)(2,1)S(1)}, u32[]{:S(2)}, u32[]{:S(2)}) collective-permute-start(bf16[8,16,384]{2,1,0:T(8,128)(2,1)S(1)} %get-tuple-element.29), channel_id=1, source_target_pairs={{0,16},{16,0},{32,48},{48,32},{64,80},{80,64},{96,112},{112,96},{1... | collective-permute-start | bytes 294920 | tf_op jit(solution)/shard_map/ppermute | solution.py:616
  28.7 0.7 collective-permute-start.5
  29.3 6.1 %shard_map.90 = (bf16[48,16,384]{2,1,0:T(8,128)(2,1)S(1)}, f32[2,3,640,128]{3,2,1,0:T(8,128)S(1)}, f32[3,40,128]{2,1,0:T(8,128)S(1)}, f32[3,3,512,128]{3,2,1,0:T(8,128)S(1)}) custom-call(s32[2,2]{1,0:T(2,128)S(1)} %copy-done.7, bf16[512,256]{1,0:T(8,128)(2,1)S(1)} %bitcast.13, bf16[272,256]{1,0:T(8,128)(2,1)S(1)} %collective-permute-done.xe_ref, ...), custom_call_target="tpu_custom_call" | custom-call | tf_op jit(solution)/shard_map/pallas_call | solution.py:683
  35.5 0.0 copy-start.5
  35.5 0.0 copy-start.6
  35.5 3.4 %shard_map.91 = (f32[3,3,640,128]{3,2,1,0:T(8,128)S(1)}, f32[8,128]{1,0:T(8,128)S(1)}) custom-call(s32[2,2]{1,0:T(2,128)S(1)} %copy-done.7, bf16[8,16,384]{2,1,0:T(8,128)(2,1)S(1)} %collective-permute-done.4.we_ref, bf16[8,16,384]{2,1,0:T(8,128)(2,1)S(1)} %collective-permute-done.5.wo_ref, bf16[48,16,384]{2,1,0:T(8,128)(2,1)S(1)} %get-tuple-element.32.fx_ref, ...), custom_call_target="tpu_custom_call" | custom-call | tf_op jit(solution)/shard_map/pallas_call | solution.py:697
  38.9 0.3 collective-permute-start.8
  39.2 5.3 %shard_map.92 = (f32[3,32,16,256]{3,2,1,0:T(8,128)S(1)}, bf16[3,7,16,256]{3,2,1,0:T(8,128)(2,1)S(1)}, bf16[3,7,16,256]{3,2,1,0:T(8,128)(2,1)S(1)}) custom-call(f32[3,3,640,128]{3,2,1,0:T(8,128)S(1)} %get-tuple-element.36.a_ref, bf16[32,16,384]{2,1,0:T(8,128)(2,1)S(1)} %get-tuple-element.31.w_ref, bf16[48,16,384]{2,1,0:T(8,128)(2,1)S(1)} %get-tuple-element.32.fx_ref, ...), custom_call_target="tpu_custom_call" | custom-call | tf_op jit(solution)/shard_map/pallas_call | solution.py:710
  44.5 8.1 %collective-permute-start.6 = (bf16[3,7,16,256]{3,2,1,0:T(8,128)(2,1)S(1)}, bf16[3,7,16,256]{3,2,1,0:T(8,128)(2,1)S(1)}, u32[]{:S(2)}, u32[]{:S(2)}) collective-permute-start(bf16[3,7,16,256]{3,2,1,0:T(8,128)(2,1)S(1)} %get-tuple-element.39), channel_id=1, source_target_pairs={{0,16},{16,0},{32,48},{48,32},{64,80},{80,64},{96,112},{112,96},{1... | collective-permute-start | bytes 516104 | tf_op jit(solution)/shard_map/ppermute | solution.py:616
  52.6 0.7 collective-permute-start.7
  53.3 30.5 %all_to_all.5 = f32[128,1,128]{2,1,0:T(1,128)S(1)} all-to-all(f32[128,1,128]{2,1,0:T(1,128)S(1)} %broadcast_in_dim.8), channel_id=1, replica_groups={{0,2,4,6,8,10,12,14,16,18,20,22,24,26,28,30,32,34,36,38,40,42,44,46,48,..., dimensions={0} | all-to-all | bytes 131072 | tf_op jit(solution)/shard_map/all_to_all | solution.py:724
  83.8 4.3 %shard_map.93 = (f32[3,512,256]{2,1,0:T(8,128)}, f32[1,128]{1,0:T(1,128)}) custom-call(f32[3,32,16,256]{3,2,1,0:T(8,128)S(1)} %get-tuple-element.38.ys_ref, bf16[3,7,16,256]{3,2,1,0:T(8,128)(2,1)S(1)} %collective-permute-done.6.ge_ref, bf16[3,7,16,256]{3,2,1,0:T(8,128)(2,1)S(1)} %collective-permute-done.7.go_ref, f32[128,128]{1,0:T(8,128)S(1)} %bitcast.17), custom_call_target="tpu_custom_call" | custom-call | tf_op jit(solution)/shard_map/pallas_call | solution.py:729
  (22 shorter events, 0.1 us)
Async XLA Ops:
  0.6 7.3 %copy-start.7 = (s32[2,2]{1,0:T(2,128)S(1)}, s32[2,2]{1,0:T(2,128)}, u32[]{:S(2)}) copy-start(s32[2,2]{1,0:T(2,128)} %t_ref.5) | copy-start | bytes 52
  0.6 7.3 %copy-start.3 = (bf16[16,32,256]{2,1,0:T(8,128)(2,1)S(1)}, bf16[16,32,256]{2,1,0:T(8,128)(2,1)}, u32[]{:S(2)}) copy-start(bf16[16,32,256]{2,1,0:T(8,128)(2,1)} %param.8) | copy-start | bytes 786436
  0.6 7.3 %copy-start.4 = (bf16[16,32,256]{2,1,0:T(8,128)(2,1)S(1)}, bf16[16,32,256]{2,1,0:T(8,128)(2,1)}, u32[]{:S(2)}) copy-start(bf16[16,32,256]{2,1,0:T(8,128)(2,1)} %param.7) | copy-start | bytes 786436
  2.5 5.4 %collective-permute-start = (bf16[272,256]{1,0:T(8,128)(2,1)}, bf16[272,256]{1,0:T(8,128)(2,1)S(1)}, u32[]{:S(2)}, u32[]{:S(2)}) collective-permute-start(bf16[272,256]{1,0:T(8,128)(2,1)} %get-tuple-element.23), channel_id=1, source_target_pairs={{0,16},{16,0},{32,48},{48,32},{64,80},{80,64},{96,112},{112,96},{1... | collective-permute-start | bytes 417800 | tf_op jit(solution)/shard_map/ppermute | solution.py:616
  4.6 3.3 %collective-permute-start.1 = (bf16[272,256]{1,0:T(8,128)(2,1)}, bf16[272,256]{1,0:T(8,128)(2,1)S(1)}, u32[]{:S(2)}, u32[]{:S(2)}) collective-permute-start(bf16[272,256]{1,0:T(8,128)(2,1)} %get-tuple-element.24), channel_id=1, source_target_pairs={{16,32},{32,16},{48,64},{64,48},{80,96},{96,80},{112,128},{128,112... | collective-permute-start | bytes 417800 | tf_op jit(solution)/shard_map/ppermute | solution.py:617
  6.1 1.4 %copy-start = (f32[3,16,32,256]{3,2,1,0:T(8,128)S(1)}, f32[3,16,32,256]{3,2,1,0:T(8,128)}, u32[]{:S(2)}) copy-start(f32[3,16,32,256]{3,2,1,0:T(8,128)} %param.9) | copy-start | bytes 4718596
  7.5 11.3 %copy-start.1 = (f32[3,16,32,256]{3,2,1,0:T(8,128)S(1)}, f32[3,16,32,256]{3,2,1,0:T(8,128)}, u32[]{:S(2)}) copy-start(f32[3,16,32,256]{3,2,1,0:T(8,128)} %param.9) | copy-start | bytes 4718596
  7.9 21.4 %copy-start.2 = (bf16[384,384]{1,0:T(8,128)(2,1)S(1)}, bf16[384,384]{1,0:T(8,128)(2,1)}, u32[]{:S(2)}) copy-start(bf16[384,384]{1,0:T(8,128)(2,1)} %constant.8.band_ref) | copy-start | bytes 884740
  8.8 5.1 %collective-permute-start.2 = (bf16[688,128]{1,0:T(8,128)(2,1)S(1)}, bf16[688,128]{1,0:T(8,128)(2,1)S(1)}, u32[]{:S(2)}, u32[]{:S(2)}) collective-permute-start(bf16[688,128]{1,0:T(8,128)(2,1)S(1)} %get-tuple-element.27), channel_id=1, source_target_pairs={{0,1},{1,0},{2,3},{3,2},{4,5},{5,4},{6,7},{7,6},{8,9},{9,8},{10,11... | collective-permute-start | bytes 528392 | tf_op jit(solution)/shard_map/ppermute | solution.py:616
  12.0 6.8 %collective-permute-start.3 = (bf16[688,128]{1,0:T(8,128)(2,1)S(1)}, bf16[688,128]{1,0:T(8,128)(2,1)S(1)}, u32[]{:S(2)}, u32[]{:S(2)}) collective-permute-start(bf16[688,128]{1,0:T(8,128)(2,1)S(1)} %get-tuple-element.28), channel_id=1, source_target_pairs={{1,2},{2,1},{3,4},{4,3},{5,6},{6,5},{7,8},{8,7},{9,10},{10,9},{11,... | collective-permute-start | bytes 528392 | tf_op jit(solution)/shard_map/ppermute | solution.py:617
  24.9 10.5 %collective-permute-start.4 = (bf16[8,16,384]{2,1,0:T(8,128)(2,1)S(1)}, bf16[8,16,384]{2,1,0:T(8,128)(2,1)S(1)}, u32[]{:S(2)}, u32[]{:S(2)}) collective-permute-start(bf16[8,16,384]{2,1,0:T(8,128)(2,1)S(1)} %get-tuple-element.29), channel_id=1, source_target_pairs={{0,16},{16,0},{32,48},{48,32},{64,80},{80,64},{96,112},{112,96},{1... | collective-permute-start | bytes 294920 | tf_op jit(solution)/shard_map/ppermute | solution.py:616
  28.7 6.8 %collective-permute-start.5 = (bf16[8,16,384]{2,1,0:T(8,128)(2,1)S(1)}, bf16[8,16,384]{2,1,0:T(8,128)(2,1)S(1)}, u32[]{:S(2)}, u32[]{:S(2)}) collective-permute-start(bf16[8,16,384]{2,1,0:T(8,128)(2,1)S(1)} %get-tuple-element.30), channel_id=1, source_target_pairs={{16,32},{32,16},{48,64},{64,48},{80,96},{96,80},{112,128},{128,112... | collective-permute-start | bytes 294920 | tf_op jit(solution)/shard_map/ppermute | solution.py:617
  35.5 3.7 %copy-start.5 = (bf16[384,256]{1,0:T(8,128)(2,1)S(1)}, bf16[384,256]{1,0:T(8,128)(2,1)}, u32[]{:S(2)}) copy-start(bf16[384,256]{1,0:T(8,128)(2,1)} %constant.12.gl_ref) | copy-start | bytes 589828
  35.5 3.7 %copy-start.6 = (bf16[384,256]{1,0:T(8,128)(2,1)S(1)}, bf16[384,256]{1,0:T(8,128)(2,1)}, u32[]{:S(2)}) copy-start(bf16[384,256]{1,0:T(8,128)(2,1)} %constant.9.gh_ref) | copy-start | bytes 589828
  38.9 14.3 %collective-permute-start.8 = (f32[8,128]{1,0:T(8,128)S(1)}, f32[8,128]{1,0:T(8,128)S(1)}, u32[]{:S(2)}, u32[]{:S(2)}) collective-permute-start(f32[8,128]{1,0:T(8,128)S(1)} %get-tuple-element.41), channel_id=1, source_target_pairs={{0,1},{1,0},{2,3},{3,2},{4,5},{5,4},{6,7},{7,6},{8,9},{9,8},{10,11... | collective-permute-start | bytes 12296 | tf_op jit(solution)/shard_map/ppermute | solution.py:720
  44.5 39.3 %collective-permute-start.6 = (bf16[3,7,16,256]{3,2,1,0:T(8,128)(2,1)S(1)}, bf16[3,7,16,256]{3,2,1,0:T(8,128)(2,1)S(1)}, u32[]{:S(2)}, u32[]{:S(2)}) collective-permute-start(bf16[3,7,16,256]{3,2,1,0:T(8,128)(2,1)S(1)} %get-tuple-element.39), channel_id=1, source_target_pairs={{0,16},{16,0},{32,48},{48,32},{64,80},{80,64},{96,112},{112,96},{1... | collective-permute-start | bytes 516104 | tf_op jit(solution)/shard_map/ppermute | solution.py:616
  52.6 31.2 %collective-permute-start.7 = (bf16[3,7,16,256]{3,2,1,0:T(8,128)(2,1)S(1)}, bf16[3,7,16,256]{3,2,1,0:T(8,128)(2,1)S(1)}, u32[]{:S(2)}, u32[]{:S(2)}) collective-permute-start(bf16[3,7,16,256]{3,2,1,0:T(8,128)(2,1)S(1)} %get-tuple-element.40), channel_id=1, source_target_pairs={{16,32},{32,16},{48,64},{64,48},{80,96},{96,80},{112,128},{128,112... | collective-permute-start | bytes 516104 | tf_op jit(solution)/shard_map/ppermute | solution.py:617

commit v3 on v2

--- a/solution.py
+++ b/solution.py
@@ -223,14 +223,14 @@
     lane = lane_iota((DEPTH, LANES))
 
     def gather(j, xb, oz, ox, oy, merge):
+        nbr = jnp.where(oy >= 0, (j + 1) % 3, (j + 2) % 3)
         shifts = []
         for b in range(2):
             s = oy + b
-            nbr = jnp.where(s >= 0, (j + 1) % 3, (j + 2) % 3)
             lo = jnp.where(s >= 0, 0, LANES + s)
             hi = jnp.where(s >= 0, s, LANES)
             mask = (lane >= lo) & (lane < hi)
-            shifts.append((nbr, mask, (LANES - s) & (LANES - 1)))
+            shifts.append((mask, (LANES - s) & (LANES - 1)))
         base = (3 + oz) * EXT + xb * BX + 8 + ox
 
         @unrolled(BX + 1)
@@ -238,16 +238,16 @@
             for c in range(2):
                 start = base + c * EXT + x
                 own = m_scr[j, pl.ds(start, DEPTH, stride=EXT), :]
+                other = m_scr[nbr, pl.ds(start, DEPTH, stride=EXT), :]
                 for b in range(2):
-                    nbr, mask, amount = shifts[b]
-                    other = m_scr[nbr, pl.ds(start, DEPTH, stride=EXT), :]
+                    mask, amount = shifts[b]
                     val = pltpu.roll(jnp.where(mask, other, own), amount, 1)
                     if merge:
                         val = jnp.where(lane < LANES // 2, r_scr[b, c, x], val)
                     r_scr[b, c, x] = val
 
     def blend(j, xb):
-        @pl.loop(0, BX, unroll=4)
+        @pl.loop(0, BX, unroll=8)
         def _(x):
             row = xb * BX + x
             f0, f1, f2 = (v_scr[c, j, pl.ds(row, DEPTH, stride=ROWS), :] for c in range(3))
@@ -332,7 +332,7 @@
 
 
 def box_z(src, dst, q, count):
-    @pl.loop(0, count // 8)
+    @unrolled(count // 8)
     def _(t):
         for j in range(3):
             rows = [pl.ds(t * 128 + z, 8, stride=DEPTH) for z in range(DEPTH)]
@@ -541,7 +541,7 @@
         o_ref[c] = pick(px, first, last).astype(BF16)
 
 
-def smooth_kernel(ys_ref, ge_ref, go_ref, all_ref, out_hbm, loss_ref, h_scr, z_scr, o_scr, sem):
+def smooth_kernel(ys_ref, ge_ref, go_ref, out_hbm, h_scr, z_scr, o_scr, sem):
     weights = gauss_weights()
     px = lax.axis_index("gx") & 1
     r = GAUSS_RADIUS
@@ -586,14 +586,17 @@
             )
             copy.start()
             copies.append(copy)
+    for copy in copies:
+        copy.wait()
+
+
+def loss_kernel(all_ref, loss_ref):
     column = lane_iota(all_ref.shape)
     shares = all_ref[...]
     total = jnp.sum(jnp.where(column == 0, shares, 0.0))
     blocks = jnp.sum(jnp.where(column == 1, shares, 0.0))
     row = jnp.full((1, LANES), -total) / (jnp.full((1, LANES), blocks) * float(BX * BY * DEPTH))
     loss_ref[...] = row
-    for copy in copies:
-        copy.wait()
 
 
 def call(kernel, outs, in_specs, out_specs, scratch=(), limit=VMEM_LIMIT):
@@ -724,20 +727,20 @@
     everyone = lax.all_to_all(
         jnp.broadcast_to(line, (count, 1, LANES)), ("gx", "gy"), 0, 0, axis_index_groups=groups
     )
-    everyone = everyone.reshape(count, LANES)
-
-    update, loss = call(
+    (loss,) = call(loss_kernel, [((1, LANES), F32)], [V], [V])(everyone.reshape(count, LANES))
+
+    (update,) = call(
         smooth_kernel,
-        [((3, rows, 2 * LANES), F32), ((1, LANES), F32)],
-        [V] * 4,
-        [A, V],
+        [((3, rows, 2 * LANES), F32)],
+        [V] * 3,
+        [A],
         [
             pltpu.VMEM((2, 3, GAUSS_RADIUS, DEPTH, 2 * LANES), F32),
             pltpu.VMEM((rows, LANES), F32),
             pltpu.VMEM((3, 2, rows, LANES), F32),
             pltpu.SemaphoreType.DMA((6,)),
         ],
-    )(ys, rge, rgo, everyone)
+    )(ys, rge, rgo)
     return update.reshape(velocity.shape), loss[0, 0]
 
 

time: 88.6 us -> 87.7 us (0.990)
  Pallas kernels: 28.4 us -> 27.2 us
    pallas_call x1, Pallas kernels: 6.15 us -> 5.23 us  [step(): call(warp_kernel, [((ROWS, DEPTH, 3 * LANES), BF16), ((3, ROWS, DEPTH, 3...]
    pallas_call x1 -> x2, Pallas kernels: 4.31 us -> 4.45 us  [the longest x1 3.8 us: step(): call(smooth_kernel, [((3, rows, 2 * LANES), F32)], [V] * 3, [A], [pltpu.V...]
  transfers between devices with their start and end apart: 9 -> 9, of which waited for: 1 -> 1; matrix products, arithmetic and copies ran while one was open for 1% -> 1% of each run, Pallas kernels for 13% -> 14%
where the time goes in v3:
time: 87.7 us; the launch traced here: 87.4 us
  blocking collectives  30.5 us (35%)
  Pallas kernels  27.2 us (31%)
  starting transfers between devices  21.5 us (25%)
  waiting for transfers between devices  4.85 us (6%)
  local copies, waits for them, and re-layouts  2.26 us (3%)
  between operations  1.06 us (1%)
    all_to_all x1, blocking collectives, step(): lax.all_to_all(jnp.broadcast_to(line, (count, 1, LANES)), ('gx', 'gy'), 0...  30.5 us
    ppermute x4, starting transfers between devices, swap(): even = lax.ppermute(even, axis, first)  17.3 us
    pallas_call x1, Pallas kernels, step(): call(window_kernel, [((EXT, DEPTH, 3 * LANES), BF16), ((2, 3, DEPTH * OUT...  5.99 us
    pallas_call x1, Pallas kernels, step(): call(warp_kernel, [((ROWS, DEPTH, 3 * LANES), BF16), ((3, ROWS, DEPTH, 3...  5.23 us
    pallas_call x1, Pallas kernels, step(): call(gradient_kernel, [((3, ROWS, DEPTH, 2 * LANES), F32), edge, edge], [...  5.15 us
    ppermute x4, waiting for transfers between devices, swap(): odd = lax.ppermute(odd, axis, second)  4.84 us
    ppermute x4, starting transfers between devices, swap(): odd = lax.ppermute(odd, axis, second)  4.06 us
    pallas_call x1, Pallas kernels, step(): call(smooth_kernel, [((3, rows, 2 * LANES), F32)], [V] * 3, [A], [pltpu.V...  3.8 us
  transfers between devices with their start and end apart: 9, of which 1 were waited for; matrix products, arithmetic and copies ran while one was open for 1% of the time, Pallas kernels for 14%

profile of v3, /device:TPU:1, one launch (start us, length us, event | category | flops | bytes accessed | tf_op | source)
XLA Modules:
  0.0 87.4 jit_solution(16058645728913622730)
XLA Ops:
  0.7 1.8 %shard_map.86 = (bf16[272,256]{1,0:T(8,128)(2,1)}, bf16[272,256]{1,0:T(8,128)(2,1)}) custom-call(s32[2,2]{1,0:T(2,128)} %t_ref.5, bf16[512,256]{1,0:T(8,128)(2,1)} %bitcast.14, bf16[512,256]{1,0:T(8,128)(2,1)} %bitcast.11), custom_call_target="tpu_custom_call" | custom-call | tf_op jit(solution)/shard_map/pallas_call | solution.py:647
  2.5 2.1 %collective-permute-start = (bf16[272,256]{1,0:T(8,128)(2,1)}, bf16[272,256]{1,0:T(8,128)(2,1)S(1)}, u32[]{:S(2)}, u32[]{:S(2)}) collective-permute-start(bf16[272,256]{1,0:T(8,128)(2,1)} %get-tuple-element.21), channel_id=1, source_target_pairs={{0,16},{16,0},{32,48},{48,32},{64,80},{80,64},{96,112},{112,96},{1... | collective-permute-start | bytes 417800 | tf_op jit(solution)/shard_map/ppermute | solution.py:619
  4.6 0.7 collective-permute-start.1
  5.3 0.8 copy.12.off_ref
  6.1 1.4 %copy-done = f32[3,16,32,256]{3,2,1,0:T(8,128)S(1)} copy-done((f32[3,16,32,256]{3,2,1,0:T(8,128)S(1)}, f32[3,16,32,256]{3,2,1,0:T(8,128)}, u32[]{:S(2)}) %copy-start) | copy-done | bytes 1572888
  7.5 0.4 shard_map.87
  7.9 0.0 copy-start.2
  8.0 0.9 shard_map.88
  8.8 3.2 %collective-permute-start.2 = (bf16[688,128]{1,0:T(8,128)(2,1)S(1)}, bf16[688,128]{1,0:T(8,128)(2,1)S(1)}, u32[]{:S(2)}, u32[]{:S(2)}) collective-permute-start(bf16[688,128]{1,0:T(8,128)(2,1)S(1)} %get-tuple-element.25), channel_id=1, source_target_pairs={{0,1},{1,0},{2,3},{3,2},{4,5},{5,4},{6,7},{7,6},{8,9},{9,8},{10,11... | collective-permute-start | bytes 528392 | tf_op jit(solution)/shard_map/ppermute | solution.py:619
  12.0 1.9 %collective-permute-start.3 = (bf16[688,128]{1,0:T(8,128)(2,1)S(1)}, bf16[688,128]{1,0:T(8,128)(2,1)S(1)}, u32[]{:S(2)}, u32[]{:S(2)}) collective-permute-start(bf16[688,128]{1,0:T(8,128)(2,1)S(1)} %get-tuple-element.26), channel_id=1, source_target_pairs={{1,2},{2,1},{3,4},{4,3},{5,6},{6,5},{7,8},{8,7},{9,10},{10,9},{11,... | collective-permute-start | bytes 528392 | tf_op jit(solution)/shard_map/ppermute | solution.py:620
  14.0 4.8 %collective-permute-done.3.yo_ref = bf16[688,128]{1,0:T(8,128)(2,1)S(1)} collective-permute-done((bf16[688,128]{1,0:T(8,128)(2,1)S(1)}, bf16[688,128]{1,0:T(8,128)(2,1)S(1)}, u32[]{:S(2)}, u32[]{:S(2)}) %collective-permute-start.3) | collective-permute-done | bytes 176160 | tf_op jit(solution)/shard_map/ppermute | solution.py:620
  18.8 5.2 %shard_map.89 = (bf16[32,16,384]{2,1,0:T(8,128)(2,1)S(1)}, f32[3,32,16,384]{3,2,1,0:T(8,128)S(1)}, bf16[8,16,384]{2,1,0:T(8,128)(2,1)S(1)}, bf16[8,16,384]{2,1,0:T(8,128)(2,1)S(1)}) custom-call(s32[3,2,2]{2,1,0:T(2,128)S(1)} %copy.12.off_ref, bf16[512,256]{1,0:T(8,128)(2,1)S(1)} %bitcast.16, bf16[272,256]{1,0:T(8,128)(2,1)S(1)} %collective-permute-done.xe_ref, ...), custom_call_target="tpu_custom_call" | custom-call | tf_op jit(solution)/shard_map/pallas_call | solution.py:670
  24.0 3.7 %collective-permute-start.4 = (bf16[8,16,384]{2,1,0:T(8,128)(2,1)S(1)}, bf16[8,16,384]{2,1,0:T(8,128)(2,1)S(1)}, u32[]{:S(2)}, u32[]{:S(2)}) collective-permute-start(bf16[8,16,384]{2,1,0:T(8,128)(2,1)S(1)} %get-tuple-element.27), channel_id=1, source_target_pairs={{0,16},{16,0},{32,48},{48,32},{64,80},{80,64},{96,112},{112,96},{1... | collective-permute-start | bytes 294920 | tf_op jit(solution)/shard_map/ppermute | solution.py:619
  27.7 0.8 collective-permute-start.5
  28.6 6.0 %shard_map.90 = (bf16[48,16,384]{2,1,0:T(8,128)(2,1)S(1)}, f32[2,3,640,128]{3,2,1,0:T(8,128)S(1)}, f32[3,40,128]{2,1,0:T(8,128)S(1)}, f32[3,3,512,128]{3,2,1,0:T(8,128)S(1)}) custom-call(s32[2,2]{1,0:T(2,128)S(1)} %copy-done.7, bf16[512,256]{1,0:T(8,128)(2,1)S(1)} %bitcast.13, bf16[272,256]{1,0:T(8,128)(2,1)S(1)} %collective-permute-done.xe_ref, ...), custom_call_target="tpu_custom_call" | custom-call | tf_op jit(solution)/shard_map/pallas_call | solution.py:686
  34.6 0.0 copy-start.5
  34.6 3.3 %shard_map.91 = (f32[3,3,640,128]{3,2,1,0:T(8,128)S(1)}, f32[8,128]{1,0:T(8,128)S(1)}) custom-call(s32[2,2]{1,0:T(2,128)S(1)} %copy-done.7, bf16[8,16,384]{2,1,0:T(8,128)(2,1)S(1)} %collective-permute-done.4.we_ref, bf16[8,16,384]{2,1,0:T(8,128)(2,1)S(1)} %collective-permute-done.5.wo_ref, bf16[48,16,384]{2,1,0:T(8,128)(2,1)S(1)} %get-tuple-element.30.fx_ref, ...), custom_call_target="tpu_custom_call" | custom-call | tf_op jit(solution)/shard_map/pallas_call | solution.py:700
  37.9 0.1 collective-permute-start.8
  38.0 5.1 %shard_map.92 = (f32[3,32,16,256]{3,2,1,0:T(8,128)S(1)}, bf16[3,7,16,256]{3,2,1,0:T(8,128)(2,1)S(1)}, bf16[3,7,16,256]{3,2,1,0:T(8,128)(2,1)S(1)}) custom-call(f32[3,3,640,128]{3,2,1,0:T(8,128)S(1)} %get-tuple-element.34.a_ref, bf16[32,16,384]{2,1,0:T(8,128)(2,1)S(1)} %get-tuple-element.29.w_ref, bf16[48,16,384]{2,1,0:T(8,128)(2,1)S(1)} %get-tuple-element.30.fx_ref, ...), custom_call_target="tpu_custom_call" | custom-call | tf_op jit(solution)/shard_map/pallas_call | solution.py:713
  43.2 8.3 %collective-permute-start.6 = (bf16[3,7,16,256]{3,2,1,0:T(8,128)(2,1)S(1)}, bf16[3,7,16,256]{3,2,1,0:T(8,128)(2,1)S(1)}, u32[]{:S(2)}, u32[]{:S(2)}) collective-permute-start(bf16[3,7,16,256]{3,2,1,0:T(8,128)(2,1)S(1)} %get-tuple-element.37), channel_id=1, source_target_pairs={{0,16},{16,0},{32,48},{48,32},{64,80},{80,64},{96,112},{112,96},{1... | collective-permute-start | bytes 516104 | tf_op jit(solution)/shard_map/ppermute | solution.py:619
  51.5 0.7 collective-permute-start.7
  52.2 30.5 %all_to_all.5 = f32[128,1,128]{2,1,0:T(1,128)S(1)} all-to-all(f32[128,1,128]{2,1,0:T(1,128)S(1)} %broadcast_in_dim.8), channel_id=1, replica_groups={{0,2,4,6,8,10,12,14,16,18,20,22,24,26,28,30,32,34,36,38,40,42,44,46,48,..., dimensions={0} | all-to-all | bytes 131072 | tf_op jit(solution)/shard_map/all_to_all | solution.py:727
  82.7 0.7 shard_map.94
  83.4 3.8 %shard_map.93 = f32[3,512,256]{2,1,0:T(8,128)} custom-call(f32[3,32,16,256]{3,2,1,0:T(8,128)S(1)} %get-tuple-element.36.ys_ref, bf16[3,7,16,256]{3,2,1,0:T(8,128)(2,1)S(1)} %collective-permute-done.6.ge_ref, bf16[3,7,16,256]{3,2,1,0:T(8,128)(2,1)S(1)} %collective-permute-done.7.go_ref), custom_call_target="tpu_custom_call" | custom-call | tf_op jit(solution)/shard_map/pallas_call | solution.py:732
  (23 shorter events, 0.1 us)
Async XLA Ops:
  0.6 7.3 %copy-start.7 = (s32[2,2]{1,0:T(2,128)S(1)}, s32[2,2]{1,0:T(2,128)}, u32[]{:S(2)}) copy-start(s32[2,2]{1,0:T(2,128)} %t_ref.5) | copy-start | bytes 52
  0.6 7.3 %copy-start.3 = (bf16[16,32,256]{2,1,0:T(8,128)(2,1)S(1)}, bf16[16,32,256]{2,1,0:T(8,128)(2,1)}, u32[]{:S(2)}) copy-start(bf16[16,32,256]{2,1,0:T(8,128)(2,1)} %param.8) | copy-start | bytes 786436
  0.7 7.3 %copy-start.4 = (bf16[16,32,256]{2,1,0:T(8,128)(2,1)S(1)}, bf16[16,32,256]{2,1,0:T(8,128)(2,1)}, u32[]{:S(2)}) copy-start(bf16[16,32,256]{2,1,0:T(8,128)(2,1)} %param.7) | copy-start | bytes 786436
  2.5 5.4 %collective-permute-start = (bf16[272,256]{1,0:T(8,128)(2,1)}, bf16[272,256]{1,0:T(8,128)(2,1)S(1)}, u32[]{:S(2)}, u32[]{:S(2)}) collective-permute-start(bf16[272,256]{1,0:T(8,128)(2,1)} %get-tuple-element.21), channel_id=1, source_target_pairs={{0,16},{16,0},{32,48},{48,32},{64,80},{80,64},{96,112},{112,96},{1... | collective-permute-start | bytes 417800 | tf_op jit(solution)/shard_map/ppermute | solution.py:619
  4.6 3.3 %collective-permute-start.1 = (bf16[272,256]{1,0:T(8,128)(2,1)}, bf16[272,256]{1,0:T(8,128)(2,1)S(1)}, u32[]{:S(2)}, u32[]{:S(2)}) collective-permute-start(bf16[272,256]{1,0:T(8,128)(2,1)} %get-tuple-element.22), channel_id=1, source_target_pairs={{16,32},{32,16},{48,64},{64,48},{80,96},{96,80},{112,128},{128,112... | collective-permute-start | bytes 417800 | tf_op jit(solution)/shard_map/ppermute | solution.py:620
  6.1 1.4 %copy-start = (f32[3,16,32,256]{3,2,1,0:T(8,128)S(1)}, f32[3,16,32,256]{3,2,1,0:T(8,128)}, u32[]{:S(2)}) copy-start(f32[3,16,32,256]{3,2,1,0:T(8,128)} %param.9) | copy-start | bytes 4718596
  7.5 11.3 %copy-start.1 = (f32[3,16,32,256]{3,2,1,0:T(8,128)S(1)}, f32[3,16,32,256]{3,2,1,0:T(8,128)}, u32[]{:S(2)}) copy-start(f32[3,16,32,256]{3,2,1,0:T(8,128)} %param.9) | copy-start | bytes 4718596
  7.9 20.7 %copy-start.2 = (bf16[384,384]{1,0:T(8,128)(2,1)S(1)}, bf16[384,384]{1,0:T(8,128)(2,1)}, u32[]{:S(2)}) copy-start(bf16[384,384]{1,0:T(8,128)(2,1)} %constant.8.band_ref) | copy-start | bytes 884740
  8.8 5.1 %collective-permute-start.2 = (bf16[688,128]{1,0:T(8,128)(2,1)S(1)}, bf16[688,128]{1,0:T(8,128)(2,1)S(1)}, u32[]{:S(2)}, u32[]{:S(2)}) collective-permute-start(bf16[688,128]{1,0:T(8,128)(2,1)S(1)} %get-tuple-element.25), channel_id=1, source_target_pairs={{0,1},{1,0},{2,3},{3,2},{4,5},{5,4},{6,7},{7,6},{8,9},{9,8},{10,11... | collective-permute-start | bytes 528392 | tf_op jit(solution)/shard_map/ppermute | solution.py:619
  12.0 6.8 %collective-permute-start.3 = (bf16[688,128]{1,0:T(8,128)(2,1)S(1)}, bf16[688,128]{1,0:T(8,128)(2,1)S(1)}, u32[]{:S(2)}, u32[]{:S(2)}) collective-permute-start(bf16[688,128]{1,0:T(8,128)(2,1)S(1)} %get-tuple-element.26), channel_id=1, source_target_pairs={{1,2},{2,1},{3,4},{4,3},{5,6},{6,5},{7,8},{8,7},{9,10},{10,9},{11,... | collective-permute-start | bytes 528392 | tf_op jit(solution)/shard_map/ppermute | solution.py:620
  24.0 10.6 %collective-permute-start.4 = (bf16[8,16,384]{2,1,0:T(8,128)(2,1)S(1)}, bf16[8,16,384]{2,1,0:T(8,128)(2,1)S(1)}, u32[]{:S(2)}, u32[]{:S(2)}) collective-permute-start(bf16[8,16,384]{2,1,0:T(8,128)(2,1)S(1)} %get-tuple-element.27), channel_id=1, source_target_pairs={{0,16},{16,0},{32,48},{48,32},{64,80},{80,64},{96,112},{112,96},{1... | collective-permute-start | bytes 294920 | tf_op jit(solution)/shard_map/ppermute | solution.py:619
  27.7 6.9 %collective-permute-start.5 = (bf16[8,16,384]{2,1,0:T(8,128)(2,1)S(1)}, bf16[8,16,384]{2,1,0:T(8,128)(2,1)S(1)}, u32[]{:S(2)}, u32[]{:S(2)}) collective-permute-start(bf16[8,16,384]{2,1,0:T(8,128)(2,1)S(1)} %get-tuple-element.28), channel_id=1, source_target_pairs={{16,32},{32,16},{48,64},{64,48},{80,96},{96,80},{112,128},{128,112... | collective-permute-start | bytes 294920 | tf_op jit(solution)/shard_map/ppermute | solution.py:620
  34.6 3.4 %copy-start.5 = (bf16[384,256]{1,0:T(8,128)(2,1)S(1)}, bf16[384,256]{1,0:T(8,128)(2,1)}, u32[]{:S(2)}) copy-start(bf16[384,256]{1,0:T(8,128)(2,1)} %constant.12.gl_ref) | copy-start | bytes 589828
  34.6 3.4 %copy-start.6 = (bf16[384,256]{1,0:T(8,128)(2,1)S(1)}, bf16[384,256]{1,0:T(8,128)(2,1)}, u32[]{:S(2)}) copy-start(bf16[384,256]{1,0:T(8,128)(2,1)} %constant.9.gh_ref) | copy-start | bytes 589828
  37.9 14.3 %collective-permute-start.8 = (f32[8,128]{1,0:T(8,128)S(1)}, f32[8,128]{1,0:T(8,128)S(1)}, u32[]{:S(2)}, u32[]{:S(2)}) collective-permute-start(f32[8,128]{1,0:T(8,128)S(1)} %get-tuple-element.39), channel_id=1, source_target_pairs={{0,1},{1,0},{2,3},{3,2},{4,5},{5,4},{6,7},{7,6},{8,9},{9,8},{10,11... | collective-permute-start | bytes 12296 | tf_op jit(solution)/shard_map/ppermute | solution.py:723
  43.2 40.2 %collective-permute-start.6 = (bf16[3,7,16,256]{3,2,1,0:T(8,128)(2,1)S(1)}, bf16[3,7,16,256]{3,2,1,0:T(8,128)(2,1)S(1)}, u32[]{:S(2)}, u32[]{:S(2)}) collective-permute-start(bf16[3,7,16,256]{3,2,1,0:T(8,128)(2,1)S(1)} %get-tuple-element.37), channel_id=1, source_target_pairs={{0,16},{16,0},{32,48},{48,32},{64,80},{80,64},{96,112},{112,96},{1... | collective-permute-start | bytes 516104 | tf_op jit(solution)/shard_map/ppermute | solution.py:619
  51.5 31.9 %collective-permute-start.7 = (bf16[3,7,16,256]{3,2,1,0:T(8,128)(2,1)S(1)}, bf16[3,7,16,256]{3,2,1,0:T(8,128)(2,1)S(1)}, u32[]{:S(2)}, u32[]{:S(2)}) collective-permute-start(bf16[3,7,16,256]{3,2,1,0:T(8,128)(2,1)S(1)} %get-tuple-element.38), channel_id=1, source_target_pairs={{16,32},{32,16},{48,64},{64,48},{80,96},{96,80},{112,128},{128,112... | collective-permute-start | bytes 516104 | tf_op jit(solution)/shard_map/ppermute | solution.py:620
